TPU v7x, 32 devices: a whole 2x2x4 slice. The times are simulated.
32 devices in a mesh: clip: 4 (over y, core), seq: 8 (over z, x).
Axes of the slice: x: 2, y: 2, z: 4, core: 2. Of those that a mesh axis runs over, the one named last changes fastest.
Arguments:
- temporal_queries: bfloat16 [32, 128, 1152], P(('clip', 'seq')), parts along dimension 0, may hold values from -6 to 6
- temporal_keys: bfloat16 [32, 128, 1152], P(('clip', 'seq')), parts along dimension 0, may hold values from -6 to 6
- temporal_values: bfloat16 [32, 128, 1152], P(('clip', 'seq')), parts along dimension 0, may hold values from -6 to 6
- temporal_cotangent: bfloat16 [32, 128, 1152], P(('clip', 'seq')), parts along dimension 0, may hold values from -6 to 6
- cross_queries: bfloat16 [32, 128, 1152], P(('clip', 'seq')), parts along dimension 0, may hold values from -6 to 6
- cross_cotangent: bfloat16 [32, 128, 1152], P(('clip', 'seq')), parts along dimension 0, may hold values from -6 to 6
- text_keys: bfloat16 [640, 1152], P('clip'), parts along dimension 0, may hold values from -6 to 6
- text_values: bfloat16 [640, 1152], P('clip'), parts along dimension 0, may hold values from -6 to 6
- text_length: int32 [4], P('clip'), parts along dimension 0, may hold values from 80 to 160
Outputs:
- temporal_queries_grad: bfloat16 [32, 128, 1152], P(('clip', 'seq')), parts along dimension 0
- temporal_keys_grad: bfloat16 [32, 128, 1152], P(('clip', 'seq')), parts along dimension 0
- temporal_values_grad: bfloat16 [32, 128, 1152], P(('clip', 'seq')), parts along dimension 0
- cross_queries_grad: bfloat16 [32, 128, 1152], P(('clip', 'seq')), parts along dimension 0
- text_kv_grad: float32 [640, 2304], P('clip', 'seq'), parts along dimension 0
There are 4 independent parts, one for each index of `clip`. A program takes and returns all parts, laid end to end along the dimension named above; each array names one. Nothing has to cross between parts.
All inputs are finite; a program needn't handle non-finite values.
Results may differ from a plain program's by a relative error of at most 0.012.
The roundings to bfloat16 on the way count: a program that leaves them out, or rounds other values in their place, can miss the bound.
Values may be sent and summed in bfloat16 or wider, within the bound.
No kernel may reach another device: no remote copies, remote signals or barrier semaphores. Data moves between devices by JAX's collectives and lax.ppermute only.
A program may use at most 64 MiB of HBM per device.

v0:
```python
import math
from functools import partial

import jax
import jax.numpy as jnp
from jax import lax
from jax.experimental import pallas as pl
from jax.experimental.pallas import tpu as pltpu
from jax.sharding import PartitionSpec as P

HEADS = 16
AXIS = "seq"
MOST_DIRECT = 8


VMEM = pl.BlockSpec(memory_space=pltpu.VMEM)
HBM = pl.BlockSpec(memory_space=pltpu.HBM)
SMEM = pl.BlockSpec(memory_space=pltpu.SMEM)


def dot_last(a, b):
    return lax.dot_general(a, b, (((1,), (1,)), ((), ())), preferred_element_type=jnp.float32)


def dot_first(a, b):
    return lax.dot_general(a, b, (((0,), (0,)), ((), ())), preferred_element_type=jnp.float32)


def attend_back(q, k, v, c, keep, scale):
    scores = jnp.where(keep, dot_last(k, q), -1e30)
    expo = jnp.exp((scores - jnp.max(scores, axis=0, keepdims=True)) * scale)
    weights = expo * (1.0 / jnp.sum(expo, axis=0, keepdims=True))
    rounded = weights.astype(jnp.bfloat16)
    products = dot_last(v, c)
    delta = jnp.sum(rounded.astype(jnp.float32) * products, axis=0, keepdims=True)
    sloped = (weights * (products - delta) * scale).astype(jnp.bfloat16)
    return (
        dot_first(sloped, k),
        jnp.dot(sloped, q, preferred_element_type=jnp.float32),
        jnp.dot(rounded, c, preferred_element_type=jnp.float32),
    )


def cross_kernel(n, fold, len_ref, q_ref, c_ref, k_ref, v_ref, grad_ref, stay_ref, send_ref):
    rows, width = q_ref.shape
    text = k_ref.shape[0]
    head_dim = width // HEADS
    scale = 1.0 / math.sqrt(head_dim)
    keep = lax.broadcasted_iota(jnp.int32, (text, rows), 0) < len_ref[0]
    groups = n if fold else 1
    per = HEADS // groups
    me = lax.axis_index(AXIS) if fold else 0
    for g in range(groups):
        parts = []
        for h in range(g * per, (g + 1) * per):
            cols = slice(h * head_dim, (h + 1) * head_dim)
            gq, gk, gv = attend_back(
                q_ref[:, cols], k_ref[:, cols], v_ref[:, cols], c_ref[:, cols], keep, scale
            )
            grad_ref[:, cols] = gq.astype(grad_ref.dtype)
            parts += [gk, gv]
        if not fold:
            for i, part in enumerate(parts):
                stay_ref[:, i * head_dim : (i + 1) * head_dim] = part
            continue
        block = jnp.concatenate(parts, axis=1)
        span = text // fold
        block = jnp.concatenate([block[i * span : (i + 1) * span] for i in range(fold)], axis=1)
        place = me ^ g

        @pl.when(place % 2 == 0)
        def _():
            stay_ref[place // 2] = block

        @pl.when(place % 2 == 1)
        def _():
            send_ref[place // 2] = block.astype(send_ref.dtype)


def temporal_kernel(slots, lanes, *refs):
    ins, outs = refs[:slots], refs[slots:]
    each, width = ins[0].shape[1:]
    rows = each * slots
    head_dim = width // HEADS
    scale = 1.0 / math.sqrt(head_dim)
    keep = (
        lax.broadcasted_iota(jnp.int32, (rows, rows), 0) % lanes
        == lax.broadcasted_iota(jnp.int32, (rows, rows), 1) % lanes
    )
    whole = [jnp.concatenate([ref[t] for ref in ins], axis=0) for t in range(4)]
    for h in range(HEADS):
        cols = slice(h * head_dim, (h + 1) * head_dim)
        q, k, v, c = (x[:, cols] for x in whole)
        for t, grad in enumerate(attend_back(q, k, v, c, keep, scale)):
            grad = grad.astype(jnp.bfloat16)
            for i, ref in enumerate(outs):
                ref[t, :, cols] = grad[i * each : (i + 1) * each]


def pack_kernel(slots, *refs):
    ins, outs, sems = refs[:4], refs[4:-1], refs[-1]
    each = ins[0].shape[0] // slots
    me = lax.axis_index(AXIS)
    copies = []
    for k, out in enumerate(outs):
        start = pl.multiple_of((me ^ k) * each, each)
        for t, ref in enumerate(ins):
            copies.append(
                pltpu.make_async_copy(ref.at[pl.ds(start, each)], out.at[t], sems.at[k, t])
            )
    for copy in copies:
        copy.start()
    for copy in copies:
        copy.wait()


def unpack_kernel(slots, fold, *refs):
    ins, (kept, got), outs = refs[:slots], refs[slots : slots + 2], refs[slots + 2 :]
    each = outs[0].shape[0] // slots
    me = lax.axis_index(AXIS)
    for k, ref in enumerate(ins):
        start = pl.multiple_of((me ^ k) * each, each)
        for t in range(3):
            outs[t][pl.ds(start, each), :] = ref[t]
    total = kept[0] + got[0].astype(jnp.float32)
    span, columns = total.shape[0], total.shape[1] // fold
    for i in range(fold):
        outs[3][i * span : (i + 1) * span, :] = total[:, i * columns : (i + 1) * columns]


PARAMS = pltpu.CompilerParams(vmem_limit_bytes=16 << 20)


def cost(flops, moved):
    return pl.CostEstimate(flops=int(flops), bytes_accessed=int(moved), transcendentals=0)


def bf16(*shape):
    return jax.ShapeDtypeStruct(shape, jnp.bfloat16)


def f32(*shape):
    return jax.ShapeDtypeStruct(shape, jnp.float32)


def local(n, tq, tk, tv, tc, cq, cc, text_k, text_v, text_len):
    frames, positions, width = tq.shape
    rows = frames * positions
    text = text_k.shape[0]
    lanes = positions // n
    columns = 2 * width // n
    fold = 128 // math.gcd(columns, 128)
    direct = (
        frames == 1
        and n <= MOST_DIRECT
        and n & (n - 1) == 0
        and HEADS % n == 0
        and positions % (8 * n) == 0
        and text % (8 * fold) == 0
    )
    flat = [x.reshape(rows, width) for x in (tq, tk, tv, tc)]
    big = cost(40 * rows * text * width, 12 * rows * width)

    def swap(x, k):
        return lax.ppermute(x, AXIS, [(i, i ^ k) for i in range(n)])

    def cross(fold, *text_out):
        return pl.pallas_call(
            partial(cross_kernel, n, fold),
            out_shape=(bf16(rows, width),) + text_out,
            in_specs=[SMEM] + [VMEM] * 4,
            out_specs=(VMEM,) * (1 + len(text_out)),
            cost_estimate=big,
            compiler_params=PARAMS,
            name="cross",
        )

    cross_args = (text_len, cq.reshape(rows, width), cc.reshape(rows, width), text_k, text_v)

    def temporal(messages, each):
        count = len(messages)
        return pl.pallas_call(
            partial(temporal_kernel, count, lanes),
            out_shape=tuple(bf16(3, each, width) for _ in messages),
            in_specs=[VMEM] * count,
            out_specs=(VMEM,) * count,
            cost_estimate=big,
            compiler_params=PARAMS,
            name="temporal",
        )(*messages)

    if not direct:
        packed = jnp.stack(flat).reshape(4, frames, n, lanes, width).transpose(2, 0, 1, 3, 4)
        moved = lax.all_to_all(packed, AXIS, 0, 0, tiled=True)
        moved = moved.transpose(1, 0, 2, 3, 4).reshape(4, rows, width)
        grad_cross, partials = pl.pallas_call(
            lambda *refs: cross_kernel(n, 0, *refs, None),
            out_shape=(bf16(rows, width), f32(text, 2 * width)),
            in_specs=[SMEM] + [VMEM] * 4,
            out_specs=(VMEM, VMEM),
            cost_estimate=big,
            compiler_params=PARAMS,
            name="cross",
        )(*cross_args)
        text_grad = lax.psum_scatter(partials, AXIS, scatter_dimension=1, tiled=True)
        (back,) = temporal([moved], rows)
        back = back.reshape(3, n, frames, lanes, width).transpose(1, 0, 2, 3, 4)
        back = lax.all_to_all(back, AXIS, 0, 0, tiled=True)
        back = back.transpose(1, 2, 0, 3, 4).reshape(3, frames, positions, width)
        return back[0], back[1], back[2], grad_cross.reshape(cq.shape), text_grad

    each = positions // n
    messages = pl.pallas_call(
        partial(pack_kernel, n),
        out_shape=tuple(bf16(4, each, width) for _ in range(n)),
        in_specs=[HBM] * 4,
        out_specs=(VMEM,) * n,
        scratch_shapes=[pltpu.SemaphoreType.DMA((n, 4))],
        cost_estimate=cost(0, 16 * rows * width),
        compiler_params=PARAMS,
        name="pack",
    )(*[pltpu.with_memory_space_constraint(x, pltpu.HBM) for x in flat])
    messages, cross_args = lax.optimization_barrier((messages, cross_args))
    order = sorted(range(1, n), key=lambda k: (-(k.bit_length()), k))
    came = {0: messages[0]}
    for k in order:
        came[k] = swap(messages[k], k)

    span = text // fold
    grad_cross, stay, send = cross(
        fold, f32(n // 2, span, fold * columns), bf16(n // 2, span, fold * columns)
    )(*cross_args)
    step = 1
    while True:
        got = swap(send, step)
        step *= 2
        if step == n:
            break
        both = stay + got.astype(jnp.float32)
        both = both.reshape(-1, 2, span, fold * columns)
        stay, send = both[:, 0], both[:, 1].astype(jnp.bfloat16)

    back = temporal([came[k] for k in range(n)], each)
    home = {0: back[0]}
    for k in order:
        home[k] = swap(back[k], k)
    out = pl.pallas_call(
        partial(unpack_kernel, n, fold),
        out_shape=(bf16(rows, width),) * 3 + (f32(text, columns),),
        in_specs=[VMEM] * (n + 2),
        out_specs=(VMEM,) * 4,
        cost_estimate=cost(0, 12 * rows * width),
        compiler_params=PARAMS,
        name="unpack",
    )(*[home[k] for k in range(n)], stay, got)
    return tuple(x.reshape(tq.shape) for x in out[:3]) + (grad_cross.reshape(cq.shape), out[3])


def solution(mesh):
    n = mesh.shape[AXIS]
    token = P(("clip", "seq"), None, None)

    def body(*args):
        return local(n, *args)

    step = jax.shard_map(
        body,
        mesh=mesh,
        in_specs=(token,) * 6 + (P("clip", None), P("clip", None), P("clip")),
        out_specs=(token,) * 4 + (P("clip", "seq"),),
        check_vma=False,
    )
    return step if 4 <= n <= MOST_DIRECT else step
```

profile of v0, /device:TPU:0, one launch (start us, length us, event | category | flops | bytes accessed | tf_op | source)
XLA Modules:
  0.0 82.5 jit_solution(1701047089844941677)
XLA Ops:
  1.3 0.0 copy-start
  1.3 0.0 copy-start.1
  1.3 0.0 copy-start.2
  1.3 1.6 %pack.1 = (bf16[4,16,1152]{2,1,0:T(8,128)(2,1)S(1)}, bf16[4,16,1152]{2,1,0:T(8,128)(2,1)S(1)}, bf16[4,16,1152]{2,1,0:T(8,128)(2,1)S(1)}, bf16[4,16,1152]{2,1,0:T...) custom-call(bf16[128,1152]{1,0:T(8,128)(2,1)} %bitcast.29, ...), custom_call_target="tpu_custom_call" | custom-call | bytes 2359296 | tf_op jit(solution)/shard_map/pack/pallas_call | solution.py:213
  2.9 0.0 copy-done
  2.9 0.0 copy-done.1
  2.9 0.0 copy-done.2
  2.9 0.0 copy-start.3
  2.9 1.0 %copy-done.3 = bf16[1,128,1152]{2,1,0:T(8,128)(2,1)S(1)} copy-done((bf16[1,128,1152]{2,1,0:T(8,128)(2,1)S(1)}, bf16[1,128,1152]{2,1,0:T(8,128)(2,1)}, u32[]{:S(2)}) %copy-start.3) | copy-done | bytes 294936
  3.9 9.0 %cross.1 = (bf16[128,1152]{1,0:T(8,128)(2,1)}, f32[4,40,1152]{2,1,0:T(8,128)S(1)}, bf16[4,40,1152]{2,1,0:T(8,128)(2,1)S(1)}) custom-call(s32[1]{0:T(128)S(6)} %copy.26.len_ref, bf16[128,1152]{1,0:T(8,128)(2,1)S(1)} %bitcast.25, bf16[128,1152]{1,0:T(8,128)(2,1)S(1)} %bitcast.26, bf16[160,1152]{1,0:T(8,128)(2,1)S(1)} %copy-done, bf16[160,1152]{1,0:T(8,128)(2,1)S(1)} %copy-done.1), custom_call_target="tpu_custom_call" | custom-call | flops 943718400 | bytes 1769472 | tf_op jit(solution)/shard_map/cross/pallas_call | solution.py:230
  12.9 3.0 %collective-permute-start.14 = (bf16[4,40,1152]{2,1,0:T(8,128)(2,1)S(1)}, bf16[4,40,1152]{2,1,0:T(8,128)(2,1)S(1)}, u32[]{:S(2)}, u32[]{:S(2)}) collective-permute-start(bf16[4,40,1152]{2,1,0:T(8,128)(2,1)S(1)} %get-tuple-element.71), channel_id=1, source_target_pairs={{0,1},{1,0},{2,3},{3,2},{4,5},{5,4},{6,7},{7,6},{8,9},{9,8},{10,11... | collective-permute-start | bytes 1105928 | tf_op jit(solution)/shard_map/ppermute | solution.py:165
  15.9 0.0 collective-permute-start
  15.9 2.1 %collective-permute-start.1 = (bf16[4,16,1152]{2,1,0:T(8,128)(2,1)S(1)}, bf16[4,16,1152]{2,1,0:T(8,128)(2,1)S(1)}, u32[]{:S(2)}, u32[]{:S(2)}) collective-permute-start(bf16[4,16,1152]{2,1,0:T(8,128)(2,1)S(1)} %get-tuple-element.51), channel_id=1, source_target_pairs={{0,2},{1,3},{2,0},{3,1},{4,6},{5,7},{6,4},{7,5},{8,10},{9,11},{10,... | collective-permute-start | bytes 442376 | tf_op jit(solution)/shard_map/ppermute | solution.py:165
  18.0 1.4 %collective-permute-start.2 = (bf16[4,16,1152]{2,1,0:T(8,128)(2,1)S(1)}, bf16[4,16,1152]{2,1,0:T(8,128)(2,1)S(1)}, u32[]{:S(2)}, u32[]{:S(2)}) collective-permute-start(bf16[4,16,1152]{2,1,0:T(8,128)(2,1)S(1)} %get-tuple-element.52), channel_id=1, source_target_pairs={{0,3},{1,2},{2,1},{3,0},{4,7},{5,6},{6,5},{7,4},{8,11},{9,10},{10,... | collective-permute-start | bytes 442376 | tf_op jit(solution)/shard_map/ppermute | solution.py:165
  19.4 2.6 %collective-permute-start.3 = (bf16[4,16,1152]{2,1,0:T(8,128)(2,1)S(1)}, bf16[4,16,1152]{2,1,0:T(8,128)(2,1)S(1)}, u32[]{:S(2)}, u32[]{:S(2)}) collective-permute-start(bf16[4,16,1152]{2,1,0:T(8,128)(2,1)S(1)} %get-tuple-element.53), channel_id=1, source_target_pairs={{0,4},{1,5},{2,6},{3,7},{4,0},{5,1},{6,2},{7,3},{8,12},{9,13},{10,... | collective-permute-start | bytes 442376 | tf_op jit(solution)/shard_map/ppermute | solution.py:165
  21.9 6.1 %collective-permute-done.14 = bf16[4,40,1152]{2,1,0:T(8,128)(2,1)S(1)} collective-permute-done((bf16[4,40,1152]{2,1,0:T(8,128)(2,1)S(1)}, bf16[4,40,1152]{2,1,0:T(8,128)(2,1)S(1)}, u32[]{:S(2)}, u32[]{:S(2)}) %collective-permute-start.14) | collective-permute-done | bytes 368672 | tf_op jit(solution)/shard_map/ppermute | solution.py:165
  28.0 4.5 %collective-permute-start.4 = (bf16[4,16,1152]{2,1,0:T(8,128)(2,1)S(1)}, bf16[4,16,1152]{2,1,0:T(8,128)(2,1)S(1)}, u32[]{:S(2)}, u32[]{:S(2)}) collective-permute-start(bf16[4,16,1152]{2,1,0:T(8,128)(2,1)S(1)} %get-tuple-element.54), channel_id=1, source_target_pairs={{0,5},{1,4},{2,7},{3,6},{4,1},{5,0},{6,3},{7,2},{8,13},{9,12},{10,... | collective-permute-start | bytes 442376 | tf_op jit(solution)/shard_map/ppermute | solution.py:165
  32.5 0.1 convert_add_fusion
  32.6 0.0 collective-permute-done.refs_1_
  32.6 3.6 %collective-permute-start.5 = (bf16[4,16,1152]{2,1,0:T(8,128)(2,1)S(1)}, bf16[4,16,1152]{2,1,0:T(8,128)(2,1)S(1)}, u32[]{:S(2)}, u32[]{:S(2)}) collective-permute-start(bf16[4,16,1152]{2,1,0:T(8,128)(2,1)S(1)} %get-tuple-element.55), channel_id=1, source_target_pairs={{0,6},{1,7},{2,4},{3,5},{4,2},{5,3},{6,0},{7,1},{8,14},{9,15},{10,... | collective-permute-start | bytes 442376 | tf_op jit(solution)/shard_map/ppermute | solution.py:165
  36.2 0.0 collective-permute-done.1.refs_2_
  36.2 1.1 %collective-permute-start.6 = (bf16[4,16,1152]{2,1,0:T(8,128)(2,1)S(1)}, bf16[4,16,1152]{2,1,0:T(8,128)(2,1)S(1)}, u32[]{:S(2)}, u32[]{:S(2)}) collective-permute-start(bf16[4,16,1152]{2,1,0:T(8,128)(2,1)S(1)} %get-tuple-element.56), channel_id=1, source_target_pairs={{0,7},{1,6},{2,5},{3,4},{4,3},{5,2},{6,1},{7,0},{8,15},{9,14},{10,... | collective-permute-start | bytes 442376 | tf_op jit(solution)/shard_map/ppermute | solution.py:165
  37.4 0.0 collective-permute-done.2.refs_3_
  37.4 0.1 collective-permute-start.15
  37.5 0.0 collective-permute-done.3.refs_4_
  37.5 7.1 %collective-permute-done.4.refs_5_ = bf16[4,16,1152]{2,1,0:T(8,128)(2,1)S(1)} collective-permute-done((bf16[4,16,1152]{2,1,0:T(8,128)(2,1)S(1)}, bf16[4,16,1152]{2,1,0:T(8,128)(2,1)S(1)}, u32[]{:S(2)}, u32[]{:S(2)}) %collective-permute-start.4) | collective-permute-done | bytes 147488 | tf_op jit(solution)/shard_map/ppermute | solution.py:165
  44.6 0.0 collective-permute-done.5.refs_6_
  44.6 1.0 %collective-permute-done.6.refs_7_ = bf16[4,16,1152]{2,1,0:T(8,128)(2,1)S(1)} collective-permute-done((bf16[4,16,1152]{2,1,0:T(8,128)(2,1)S(1)}, bf16[4,16,1152]{2,1,0:T(8,128)(2,1)S(1)}, u32[]{:S(2)}, u32[]{:S(2)}) %collective-permute-start.6) | collective-permute-done | bytes 147488 | tf_op jit(solution)/shard_map/ppermute | solution.py:165
  45.6 4.4 %temporal.1 = (bf16[3,16,1152]{2,1,0:T(8,128)(2,1)S(1)}, bf16[3,16,1152]{2,1,0:T(8,128)(2,1)S(1)}, bf16[3,16,1152]{2,1,0:T(8,128)(2,1)S(1)}, bf16[3,16,1152]{2,1...) custom-call(bf16[4,16,1152]{2,1,0:T(8,128)(2,1)S(1)} %get-tuple-elem, ...), custom_call_target="tpu_custom_call" | custom-call | flops 943718400 | bytes 1769472 | tf_op jit(solution)/shard_map/temporal/pallas_call | solution.py:182
  50.0 1.4 %collective-permute-start.7 = (bf16[3,16,1152]{2,1,0:T(8,128)(2,1)S(1)}, bf16[3,16,1152]{2,1,0:T(8,128)(2,1)S(1)}, u32[]{:S(2)}, u32[]{:S(2)}) collective-permute-start(bf16[3,16,1152]{2,1,0:T(8,128)(2,1)S(1)} %get-tuple-element.58), channel_id=1, source_target_pairs={{0,1},{1,0},{2,3},{3,2},{4,5},{5,4},{6,7},{7,6},{8,9},{9,8},{10,11... | collective-permute-start | bytes 331784 | tf_op jit(solution)/shard_map/ppermute | solution.py:165
  51.4 4.8 %collective-permute-start.8 = (bf16[3,16,1152]{2,1,0:T(8,128)(2,1)S(1)}, bf16[3,16,1152]{2,1,0:T(8,128)(2,1)S(1)}, u32[]{:S(2)}, u32[]{:S(2)}) collective-permute-start(bf16[3,16,1152]{2,1,0:T(8,128)(2,1)S(1)} %get-tuple-element.59), channel_id=1, source_target_pairs={{0,2},{1,3},{2,0},{3,1},{4,6},{5,7},{6,4},{7,5},{8,10},{9,11},{10,... | collective-permute-start | bytes 331784 | tf_op jit(solution)/shard_map/ppermute | solution.py:165
  56.2 0.5 collective-permute-start.9
  56.7 3.2 %collective-permute-start.10 = (bf16[3,16,1152]{2,1,0:T(8,128)(2,1)S(1)}, bf16[3,16,1152]{2,1,0:T(8,128)(2,1)S(1)}, u32[]{:S(2)}, u32[]{:S(2)}) collective-permute-start(bf16[3,16,1152]{2,1,0:T(8,128)(2,1)S(1)} %get-tuple-element.61), channel_id=1, source_target_pairs={{0,4},{1,5},{2,6},{3,7},{4,0},{5,1},{6,2},{7,3},{8,12},{9,13},{10,... | collective-permute-start | bytes 331784 | tf_op jit(solution)/shard_map/ppermute | solution.py:165
  59.9 0.0 collective-permute-done.15
  59.9 0.3 collective-permute-start.11
  60.3 0.0 collective-permute-done.7.refs_1_
  60.3 2.4 %collective-permute-start.12 = (bf16[3,16,1152]{2,1,0:T(8,128)(2,1)S(1)}, bf16[3,16,1152]{2,1,0:T(8,128)(2,1)S(1)}, u32[]{:S(2)}, u32[]{:S(2)}) collective-permute-start(bf16[3,16,1152]{2,1,0:T(8,128)(2,1)S(1)} %get-tuple-element.63), channel_id=1, source_target_pairs={{0,6},{1,7},{2,4},{3,5},{4,2},{5,3},{6,0},{7,1},{8,14},{9,15},{10,... | collective-permute-start | bytes 331784 | tf_op jit(solution)/shard_map/ppermute | solution.py:165
  62.7 0.0 collective-permute-done.8.refs_2_
  62.7 2.0 %collective-permute-start.13 = (bf16[3,16,1152]{2,1,0:T(8,128)(2,1)S(1)}, bf16[3,16,1152]{2,1,0:T(8,128)(2,1)S(1)}, u32[]{:S(2)}, u32[]{:S(2)}) collective-permute-start(bf16[3,16,1152]{2,1,0:T(8,128)(2,1)S(1)} %get-tuple-element.64), channel_id=1, source_target_pairs={{0,7},{1,6},{2,5},{3,4},{4,3},{5,2},{6,1},{7,0},{8,15},{9,14},{10,... | collective-permute-start | bytes 331784 | tf_op jit(solution)/shard_map/ppermute | solution.py:165
  64.8 0.0 collective-permute-done.9.refs_3_
  64.8 1.4 %collective-permute-start.16 = (bf16[1,40,1152]{2,1,0:T(8,128)(2,1)S(1)}, bf16[1,40,1152]{2,1,0:T(8,128)(2,1)S(1)}, u32[]{:S(2)}, u32[]{:S(2)}) collective-permute-start(bf16[1,40,1152]{2,1,0:T(8,128)(2,1)S(1)} %fusion.3), channel_id=1, source_target_pairs={{0,4},{1,5},{2,6},{3,7},{4,0},{5,1},{6,2},{7,3},{8,12},{9,13},{10,... | collective-permute-start | bytes 276488 | tf_op jit(solution)/shard_map/ppermute | solution.py:165
  66.2 7.8 %collective-permute-done.10.refs_4_ = bf16[3,16,1152]{2,1,0:T(8,128)(2,1)S(1)} collective-permute-done((bf16[3,16,1152]{2,1,0:T(8,128)(2,1)S(1)}, bf16[3,16,1152]{2,1,0:T(8,128)(2,1)S(1)}, u32[]{:S(2)}, u32[]{:S(2)}) %collective-permute-start.10) | collective-permute-done | bytes 110624 | tf_op jit(solution)/shard_map/ppermute | solution.py:165
  74.0 2.1 %collective-permute-done.11.refs_5_ = bf16[3,16,1152]{2,1,0:T(8,128)(2,1)S(1)} collective-permute-done((bf16[3,16,1152]{2,1,0:T(8,128)(2,1)S(1)}, bf16[3,16,1152]{2,1,0:T(8,128)(2,1)S(1)}, u32[]{:S(2)}, u32[]{:S(2)}) %collective-permute-start.11) | collective-permute-done | bytes 110624 | tf_op jit(solution)/shard_map/ppermute | solution.py:165
  76.1 0.0 collective-permute-done.12.refs_6_
  76.1 0.0 collective-permute-done.13.refs_7_
  76.1 5.3 %collective-permute-done.16.refs_9_ = bf16[1,40,1152]{2,1,0:T(8,128)(2,1)S(1)} collective-permute-done((bf16[1,40,1152]{2,1,0:T(8,128)(2,1)S(1)}, bf16[1,40,1152]{2,1,0:T(8,128)(2,1)S(1)}, u32[]{:S(2)}, u32[]{:S(2)}) %collective-permute-start.16) | collective-permute-done | bytes 92192 | tf_op jit(solution)/shard_map/ppermute | solution.py:165
  81.4 1.1 %unpack.1 = (bf16[128,1152]{1,0:T(8,128)(2,1)}, bf16[128,1152]{1,0:T(8,128)(2,1)}, bf16[128,1152]{1,0:T(8,128)(2,1)}, f32[160,288]{1,0:T(8,128)}) custom-call(bf16[3,16,1152]{2,1,0:T(8,128)(2,1)S(1)} %get-tuple-element.57.refs_0_, bf16[3,16,1152]{2,1,0:T(8,128)(2,1)S(1)} %collective-permute-done.7.refs_1_, ...), custom_call_target="tpu_custom_call" | custom-call | bytes 1769472 | tf_op jit(solution)/shard_map/unpack/pallas_call | solution.py:247
  (4 shorter events, 0.1 us)
Async XLA Ops:
  1.3 1.6 %copy-start = (bf16[160,1152]{1,0:T(8,128)(2,1)S(1)}, bf16[160,1152]{1,0:T(8,128)(2,1)}, u32[]{:S(2)}) copy-start(bf16[160,1152]{1,0:T(8,128)(2,1)} %k_ref) | copy-start | bytes 1105924
  1.3 1.6 %copy-start.1 = (bf16[160,1152]{1,0:T(8,128)(2,1)S(1)}, bf16[160,1152]{1,0:T(8,128)(2,1)}, u32[]{:S(2)}) copy-start(bf16[160,1152]{1,0:T(8,128)(2,1)} %v_ref) | copy-start | bytes 1105924
  1.3 1.6 %copy-start.2 = (bf16[1,128,1152]{2,1,0:T(8,128)(2,1)S(1)}, bf16[1,128,1152]{2,1,0:T(8,128)(2,1)}, u32[]{:S(2)}) copy-start(bf16[1,128,1152]{2,1,0:T(8,128)(2,1)} %param.13) | copy-start | bytes 884740
  2.9 1.0 %copy-start.3 = (bf16[1,128,1152]{2,1,0:T(8,128)(2,1)S(1)}, bf16[1,128,1152]{2,1,0:T(8,128)(2,1)}, u32[]{:S(2)}) copy-start(bf16[1,128,1152]{2,1,0:T(8,128)(2,1)} %param.14) | copy-start | bytes 884740
  12.9 15.1 %collective-permute-start.14 = (bf16[4,40,1152]{2,1,0:T(8,128)(2,1)S(1)}, bf16[4,40,1152]{2,1,0:T(8,128)(2,1)S(1)}, u32[]{:S(2)}, u32[]{:S(2)}) collective-permute-start(bf16[4,40,1152]{2,1,0:T(8,128)(2,1)S(1)} %get-tuple-element.71), channel_id=1, source_target_pairs={{0,1},{1,0},{2,3},{3,2},{4,5},{5,4},{6,7},{7,6},{8,9},{9,8},{10,11... | collective-permute-start | bytes 1105928 | tf_op jit(solution)/shard_map/ppermute | solution.py:165
  15.9 16.7 %collective-permute-start = (bf16[4,16,1152]{2,1,0:T(8,128)(2,1)S(1)}, bf16[4,16,1152]{2,1,0:T(8,128)(2,1)S(1)}, u32[]{:S(2)}, u32[]{:S(2)}) collective-permute-start(bf16[4,16,1152]{2,1,0:T(8,128)(2,1)S(1)} %get-tuple-element.50), channel_id=1, source_target_pairs={{0,1},{1,0},{2,3},{3,2},{4,5},{5,4},{6,7},{7,6},{8,9},{9,8},{10,11... | collective-permute-start | bytes 442376 | tf_op jit(solution)/shard_map/ppermute | solution.py:165
  15.9 20.3 %collective-permute-start.1 = (bf16[4,16,1152]{2,1,0:T(8,128)(2,1)S(1)}, bf16[4,16,1152]{2,1,0:T(8,128)(2,1)S(1)}, u32[]{:S(2)}, u32[]{:S(2)}) collective-permute-start(bf16[4,16,1152]{2,1,0:T(8,128)(2,1)S(1)} %get-tuple-element.51), channel_id=1, source_target_pairs={{0,2},{1,3},{2,0},{3,1},{4,6},{5,7},{6,4},{7,5},{8,10},{9,11},{10,... | collective-permute-start | bytes 442376 | tf_op jit(solution)/shard_map/ppermute | solution.py:165
  18.0 19.4 %collective-permute-start.2 = (bf16[4,16,1152]{2,1,0:T(8,128)(2,1)S(1)}, bf16[4,16,1152]{2,1,0:T(8,128)(2,1)S(1)}, u32[]{:S(2)}, u32[]{:S(2)}) collective-permute-start(bf16[4,16,1152]{2,1,0:T(8,128)(2,1)S(1)} %get-tuple-element.52), channel_id=1, source_target_pairs={{0,3},{1,2},{2,1},{3,0},{4,7},{5,6},{6,5},{7,4},{8,11},{9,10},{10,... | collective-permute-start | bytes 442376 | tf_op jit(solution)/shard_map/ppermute | solution.py:165
  19.4 18.1 %collective-permute-start.3 = (bf16[4,16,1152]{2,1,0:T(8,128)(2,1)S(1)}, bf16[4,16,1152]{2,1,0:T(8,128)(2,1)S(1)}, u32[]{:S(2)}, u32[]{:S(2)}) collective-permute-start(bf16[4,16,1152]{2,1,0:T(8,128)(2,1)S(1)} %get-tuple-element.53), channel_id=1, source_target_pairs={{0,4},{1,5},{2,6},{3,7},{4,0},{5,1},{6,2},{7,3},{8,12},{9,13},{10,... | collective-permute-start | bytes 442376 | tf_op jit(solution)/shard_map/ppermute | solution.py:165
  28.0 16.6 %collective-permute-start.4 = (bf16[4,16,1152]{2,1,0:T(8,128)(2,1)S(1)}, bf16[4,16,1152]{2,1,0:T(8,128)(2,1)S(1)}, u32[]{:S(2)}, u32[]{:S(2)}) collective-permute-start(bf16[4,16,1152]{2,1,0:T(8,128)(2,1)S(1)} %get-tuple-element.54), channel_id=1, source_target_pairs={{0,5},{1,4},{2,7},{3,6},{4,1},{5,0},{6,3},{7,2},{8,13},{9,12},{10,... | collective-permute-start | bytes 442376 | tf_op jit(solution)/shard_map/ppermute | solution.py:165
  32.6 12.0 %collective-permute-start.5 = (bf16[4,16,1152]{2,1,0:T(8,128)(2,1)S(1)}, bf16[4,16,1152]{2,1,0:T(8,128)(2,1)S(1)}, u32[]{:S(2)}, u32[]{:S(2)}) collective-permute-start(bf16[4,16,1152]{2,1,0:T(8,128)(2,1)S(1)} %get-tuple-element.55), channel_id=1, source_target_pairs={{0,6},{1,7},{2,4},{3,5},{4,2},{5,3},{6,0},{7,1},{8,14},{9,15},{10,... | collective-permute-start | bytes 442376 | tf_op jit(solution)/shard_map/ppermute | solution.py:165
  36.2 9.4 %collective-permute-start.6 = (bf16[4,16,1152]{2,1,0:T(8,128)(2,1)S(1)}, bf16[4,16,1152]{2,1,0:T(8,128)(2,1)S(1)}, u32[]{:S(2)}, u32[]{:S(2)}) collective-permute-start(bf16[4,16,1152]{2,1,0:T(8,128)(2,1)S(1)} %get-tuple-element.56), channel_id=1, source_target_pairs={{0,7},{1,6},{2,5},{3,4},{4,3},{5,2},{6,1},{7,0},{8,15},{9,14},{10,... | collective-permute-start | bytes 442376 | tf_op jit(solution)/shard_map/ppermute | solution.py:165
  37.4 22.5 %collective-permute-start.15 = (bf16[2,40,1152]{2,1,0:T(8,128)(2,1)S(1)}, bf16[2,40,1152]{2,1,0:T(8,128)(2,1)S(1)}, u32[]{:S(2)}, u32[]{:S(2)}) collective-permute-start(bf16[2,40,1152]{2,1,0:T(8,128)(2,1)S(1)} %fusion.2), channel_id=1, source_target_pairs={{0,2},{1,3},{2,0},{3,1},{4,6},{5,7},{6,4},{7,5},{8,10},{9,11},{10,... | collective-permute-start | bytes 552968 | tf_op jit(solution)/shard_map/ppermute | solution.py:165
  50.0 10.3 %collective-permute-start.7 = (bf16[3,16,1152]{2,1,0:T(8,128)(2,1)S(1)}, bf16[3,16,1152]{2,1,0:T(8,128)(2,1)S(1)}, u32[]{:S(2)}, u32[]{:S(2)}) collective-permute-start(bf16[3,16,1152]{2,1,0:T(8,128)(2,1)S(1)} %get-tuple-element.58), channel_id=1, source_target_pairs={{0,1},{1,0},{2,3},{3,2},{4,5},{5,4},{6,7},{7,6},{8,9},{9,8},{10,11... | collective-permute-start | bytes 331784 | tf_op jit(solution)/shard_map/ppermute | solution.py:165
  51.4 11.3 %collective-permute-start.8 = (bf16[3,16,1152]{2,1,0:T(8,128)(2,1)S(1)}, bf16[3,16,1152]{2,1,0:T(8,128)(2,1)S(1)}, u32[]{:S(2)}, u32[]{:S(2)}) collective-permute-start(bf16[3,16,1152]{2,1,0:T(8,128)(2,1)S(1)} %get-tuple-element.59), channel_id=1, source_target_pairs={{0,2},{1,3},{2,0},{3,1},{4,6},{5,7},{6,4},{7,5},{8,10},{9,11},{10,... | collective-permute-start | bytes 331784 | tf_op jit(solution)/shard_map/ppermute | solution.py:165
  56.2 8.6 %collective-permute-start.9 = (bf16[3,16,1152]{2,1,0:T(8,128)(2,1)S(1)}, bf16[3,16,1152]{2,1,0:T(8,128)(2,1)S(1)}, u32[]{:S(2)}, u32[]{:S(2)}) collective-permute-start(bf16[3,16,1152]{2,1,0:T(8,128)(2,1)S(1)} %get-tuple-element.60), channel_id=1, source_target_pairs={{0,3},{1,2},{2,1},{3,0},{4,7},{5,6},{6,5},{7,4},{8,11},{9,10},{10,... | collective-permute-start | bytes 331784 | tf_op jit(solution)/shard_map/ppermute | solution.py:165
  56.7 17.4 %collective-permute-start.10 = (bf16[3,16,1152]{2,1,0:T(8,128)(2,1)S(1)}, bf16[3,16,1152]{2,1,0:T(8,128)(2,1)S(1)}, u32[]{:S(2)}, u32[]{:S(2)}) collective-permute-start(bf16[3,16,1152]{2,1,0:T(8,128)(2,1)S(1)} %get-tuple-element.61), channel_id=1, source_target_pairs={{0,4},{1,5},{2,6},{3,7},{4,0},{5,1},{6,2},{7,3},{8,12},{9,13},{10,... | collective-permute-start | bytes 331784 | tf_op jit(solution)/shard_map/ppermute | solution.py:165
  59.9 16.2 %collective-permute-start.11 = (bf16[3,16,1152]{2,1,0:T(8,128)(2,1)S(1)}, bf16[3,16,1152]{2,1,0:T(8,128)(2,1)S(1)}, u32[]{:S(2)}, u32[]{:S(2)}) collective-permute-start(bf16[3,16,1152]{2,1,0:T(8,128)(2,1)S(1)} %get-tuple-element.62), channel_id=1, source_target_pairs={{0,5},{1,4},{2,7},{3,6},{4,1},{5,0},{6,3},{7,2},{8,13},{9,12},{10,... | collective-permute-start | bytes 331784 | tf_op jit(solution)/shard_map/ppermute | solution.py:165
  60.3 15.8 %collective-permute-start.12 = (bf16[3,16,1152]{2,1,0:T(8,128)(2,1)S(1)}, bf16[3,16,1152]{2,1,0:T(8,128)(2,1)S(1)}, u32[]{:S(2)}, u32[]{:S(2)}) collective-permute-start(bf16[3,16,1152]{2,1,0:T(8,128)(2,1)S(1)} %get-tuple-element.63), channel_id=1, source_target_pairs={{0,6},{1,7},{2,4},{3,5},{4,2},{5,3},{6,0},{7,1},{8,14},{9,15},{10,... | collective-permute-start | bytes 331784 | tf_op jit(solution)/shard_map/ppermute | solution.py:165
  62.7 13.4 %collective-permute-start.13 = (bf16[3,16,1152]{2,1,0:T(8,128)(2,1)S(1)}, bf16[3,16,1152]{2,1,0:T(8,128)(2,1)S(1)}, u32[]{:S(2)}, u32[]{:S(2)}) collective-permute-start(bf16[3,16,1152]{2,1,0:T(8,128)(2,1)S(1)} %get-tuple-element.64), channel_id=1, source_target_pairs={{0,7},{1,6},{2,5},{3,4},{4,3},{5,2},{6,1},{7,0},{8,15},{9,14},{10,... | collective-permute-start | bytes 331784 | tf_op jit(solution)/shard_map/ppermute | solution.py:165
  64.8 16.6 %collective-permute-start.16 = (bf16[1,40,1152]{2,1,0:T(8,128)(2,1)S(1)}, bf16[1,40,1152]{2,1,0:T(8,128)(2,1)S(1)}, u32[]{:S(2)}, u32[]{:S(2)}) collective-permute-start(bf16[1,40,1152]{2,1,0:T(8,128)(2,1)S(1)} %fusion.3), channel_id=1, source_target_pairs={{0,4},{1,5},{2,6},{3,7},{4,0},{5,1},{6,2},{7,3},{8,12},{9,13},{10,... | collective-permute-start | bytes 276488 | tf_op jit(solution)/shard_map/ppermute | solution.py:165
where the time goes:
time: 82.7 us; the launch traced here: 82.5 us
  starting transfers between devices  34.5 us (42%)
  waiting for transfers between devices  29.4 us (36%)
  Pallas kernels  16 us (19%)
  between operations  1.43 us (2%)
  local copies, waits for them, and re-layouts  1.02 us (1%)
    ppermute x17, starting transfers between devices, swap(): return lax.ppermute(x, AXIS, [(i, i ^ k) for i in range(n)])  34.5 us
    ppermute x17, waiting for transfers between devices, swap(): return lax.ppermute(x, AXIS, [(i, i ^ k) for i in range(n)])  29.4 us
    pallas_call x1, Pallas kernels, local(): cross(fold, f32(n // 2, span, fold * columns), bf16(n // 2, span, fold *...  9 us
    pallas_call x1, Pallas kernels, temporal(): pl.pallas_call(partial(temporal_kernel, count, lanes), out_shape=tuple((b...  4.39 us
  transfers between devices with their start and end apart: 17, of which 6 were waited for; matrix products, arithmetic and copies ran while one was open for 0% of the time, Pallas kernels for 5%

commit v1 on v0

v1 whole, which is shorter than its diff:
```python
import math
from functools import partial

import jax
import jax.numpy as jnp
from jax import lax
from jax.experimental import pallas as pl
from jax.experimental.pallas import tpu as pltpu
from jax.sharding import PartitionSpec as P

HEADS = 16
LANES = 128
AXIS = "seq"
MOST_DIRECT = 8


VMEM = pl.BlockSpec(memory_space=pltpu.VMEM)
HBM = pl.BlockSpec(memory_space=pltpu.HBM)
SMEM = pl.BlockSpec(memory_space=pltpu.SMEM)


def dot(a, b, along_a, along_b):
    dims = (((along_a,), (along_b,)), ((), ()))
    return lax.dot_general(a, b, dims, preferred_element_type=jnp.float32)


class Heads:
    def __init__(self, width):
        self.size = width // HEADS
        self.tiles = width // LANES
        self.masks = {}

    def mask(self, low, high):
        if (low, high) not in self.masks:
            lane = lax.broadcasted_iota(jnp.int32, (1, LANES), 1)
            inside = ((lane >= low) & (lane < high)).astype(jnp.float32)
            self.masks[low, high] = inside.astype(jnp.bfloat16)
        return self.masks[low, high]

    def touched(self, head):
        return range(head * self.size // LANES, -(-(head + 1) * self.size // LANES))

    def tile(self, x, t):
        return x[:, t * LANES : (t + 1) * LANES]

    def only(self, x, head, t):
        low = max(head * self.size - t * LANES, 0)
        high = min((head + 1) * self.size - t * LANES, LANES)
        return self.tile(x, t) * self.mask(low, high)

    def placed(self, x, head, to):
        start, out = head * self.size, {}
        for t in self.touched(head):
            turn = (to - start) % LANES
            turned = pltpu.roll(self.tile(x, t), turn, 1) if turn else self.tile(x, t)
            for u in range(to // LANES, -(-(to + self.size) // LANES)):
                low = max(0, LANES * t - start, LANES * u - to)
                high = min(self.size, LANES * (t + 1) - start, LANES * (u + 1) - to)
                if low < high:
                    part = turned * self.mask(to + low - LANES * u, to + high - LANES * u)
                    out[u] = out[u] + part if u in out else part
        return out

    def products(self, q, k, v, c, head):
        tiles = self.touched(head)
        ks = {t: self.only(k, head, t) for t in tiles}
        cs = {t: self.only(c, head, t) for t in tiles}
        scores = dot(beside(ks.values()), beside([self.tile(q, t) for t in tiles]), 1, 1)
        products = dot(beside([self.tile(v, t) for t in tiles]), beside(cs.values()), 1, 1)
        return scores, products, ks, cs


def beside(parts):
    parts = list(parts)
    return parts[0] if len(parts) == 1 else jnp.concatenate(parts, axis=1)


def below(parts):
    parts = list(parts)
    return parts[0] if len(parts) == 1 else jnp.concatenate(parts, axis=0)


def softmax_back(scores, products, keep, scale):
    scores = jnp.where(keep, scores, -1e30)
    expo = jnp.exp((scores - jnp.max(scores, axis=0, keepdims=True)) * scale)
    weights = expo * (1.0 / jnp.sum(expo, axis=0, keepdims=True))
    rounded = weights.astype(jnp.bfloat16)
    delta = jnp.sum(rounded.astype(jnp.float32) * products, axis=0, keepdims=True)
    return rounded, (weights * (products - delta) * scale).astype(jnp.bfloat16)


def attend_back(heads, q, k, v, c, keep, ahead, each_head, each_tile):
    scale = 1.0 / math.sqrt(heads.size)
    first, ready, tile = {}, {}, 0
    for step in range(HEADS + ahead):
        if step < HEADS:
            first[step] = heads.products(q, k, v, c, step)
        h = step - ahead
        if h < 0:
            continue
        scores, products, ks, cs = first.pop(h)
        rounded, sloped = softmax_back(scores, products, keep, scale)
        ready[h] = (rounded, sloped, ks, cs)
        each_head(h, rounded, sloped)
        while tile < heads.tiles and (tile + 1) * LANES <= (h + 1) * heads.size:
            parts = [
                (g, r, s, ks[tile], cs[tile])
                for g, (r, s, ks, cs) in sorted(ready.items())
                if tile in heads.touched(g)
            ]
            each_tile(tile, parts)
            ready = {g: x for g, x in ready.items() if heads.touched(g)[-1] > tile}
            tile += 1


def cross_kernel(groups, len_ref, q_ref, c_ref, k_ref, v_ref, grad_ref, *text_refs):
    rows, width = q_ref.shape
    text = k_ref.shape[0]
    heads = Heads(width)
    keep = lax.broadcasted_iota(jnp.int32, (text, rows), 0) < len_ref[0]
    q, c, k, v = q_ref[...], c_ref[...], k_ref[...], v_ref[...]
    per = HEADS // groups
    rest = 2 * per * heads.size % LANES
    terms, blocks = {}, []
    me = lax.axis_index(AXIS) if groups > 1 else 0

    def each_head(h, rounded, sloped):
        block, i = divmod(h, per)
        for left, x, to in ((sloped, q, 2 * i), (rounded, c, 2 * i + 1)):
            for t, value in heads.placed(x, h, to * heads.size).items():
                terms.setdefault(t, []).append((left, value))
        if i < per - 1:
            return
        tiles = [dot(beside(a for a, _ in x), below(b for _, b in x), 1, 0) for x in terms.values()]
        terms.clear()
        if rest:
            last, span = tiles.pop(), text * rest // LANES
            tiles.append(
                sum(
                    pltpu.roll(last[i * span : (i + 1) * span], i * rest, 1)
                    if i
                    else last[:span]
                    for i in range(LANES // rest)
                )
            )
        blocks.append(below(tiles))
        if groups == 1:
            text_refs[0][0] = blocks.pop()
        elif block % 2:
            odd, even = blocks.pop(), blocks.pop()
            place = (block // 2) ^ (me // 2)
            swapped = me % 2 == 1
            text_refs[0][place] = jnp.where(swapped, odd, even)
            text_refs[1][place] = jnp.where(swapped, even, odd).astype(jnp.bfloat16)

    def each_tile(t, parts):
        grad = dot(below(s for _, _, s, _, _ in parts), below(k for *_, k, _ in parts), 0, 0)
        grad_ref[:, t * LANES : (t + 1) * LANES] = grad.astype(jnp.bfloat16)

    attend_back(heads, q, k, v, c, keep, 6, each_head, each_tile)


def temporal_kernel(slots, lanes, *refs):
    ins, outs = refs[:slots], refs[slots:]
    each, width = ins[0].shape[1:]
    rows = each * slots
    heads = Heads(width)
    keep = (
        lax.broadcasted_iota(jnp.int32, (rows, rows), 0) % lanes
        == lax.broadcasted_iota(jnp.int32, (rows, rows), 1) % lanes
    )
    q, k, v, c = (below(ref[t] for ref in ins) for t in range(4))

    def each_tile(t, parts):
        slopes = [s for _, _, s, _, _ in parts]
        grads = (
            dot(below(slopes), below(k for *_, k, _ in parts), 0, 0),
            dot(beside(slopes), below(heads.only(q, g, t) for g, *_ in parts), 1, 0),
            dot(beside(r for _, r, *_ in parts), below(c for *_, c in parts), 1, 0),
        )
        for x, grad in enumerate(grads):
            grad = grad.astype(jnp.bfloat16)
            for i, ref in enumerate(outs):
                ref[x, :, t * LANES : (t + 1) * LANES] = grad[i * each : (i + 1) * each]

    attend_back(heads, q, k, v, c, keep, 8, lambda *_: None, each_tile)


def pack_kernel(slots, *refs):
    ins, outs, sems = refs[:4], refs[4:-1], refs[-1]
    each = ins[0].shape[0] // slots
    me = lax.axis_index(AXIS)
    copies = []
    for k, out in enumerate(outs):
        start = pl.multiple_of((me ^ k) * each, each)
        for t, ref in enumerate(ins):
            copies.append(
                pltpu.make_async_copy(ref.at[pl.ds(start, each)], out.at[t], sems.at[k, t])
            )
    for copy in copies:
        copy.start()
    for copy in copies:
        copy.wait()


def unpack_kernel(slots, *refs):
    ins, (kept, got), outs = refs[:slots], refs[slots : slots + 2], refs[slots + 2 :]
    each = outs[0].shape[0] // slots
    me = lax.axis_index(AXIS)
    for k, ref in enumerate(ins):
        start = pl.multiple_of((me ^ k) * each, each)
        for t in range(3):
            outs[t][pl.ds(start, each), :] = ref[t]
    total = kept[0] + got[0].astype(jnp.float32)
    text, columns = outs[3].shape
    whole, rest = divmod(columns, LANES)
    for t in range(whole):
        outs[3][:, t * LANES : (t + 1) * LANES] = total[t * text : (t + 1) * text]
    span = text * rest // LANES
    for i in range(LANES // rest if rest else 0):
        last = total[whole * text : whole * text + span, i * rest : (i + 1) * rest]
        outs[3][i * span : (i + 1) * span, whole * LANES :] = last


PARAMS = pltpu.CompilerParams(vmem_limit_bytes=16 << 20)


def cost(flops, moved):
    return pl.CostEstimate(flops=int(flops), bytes_accessed=int(moved), transcendentals=0)


def bf16(*shape):
    return jax.ShapeDtypeStruct(shape, jnp.bfloat16)


def f32(*shape):
    return jax.ShapeDtypeStruct(shape, jnp.float32)


def local(n, tq, tk, tv, tc, cq, cc, text_k, text_v, text_len):
    frames, positions, width = tq.shape
    rows = frames * positions
    text = text_k.shape[0]
    lanes = positions // n
    columns = 2 * width // n
    rest = columns % LANES
    direct = (
        frames == 1
        and 4 <= n <= MOST_DIRECT
        and n & (n - 1) == 0
        and HEADS % n == 0
        and positions % (8 * n) == 0
        and (rest == 0 or (LANES % rest == 0 and text * rest % (8 * LANES) == 0))
    )
    flat = [x.reshape(rows, width) for x in (tq, tk, tv, tc)]
    big = cost(40 * rows * text * width, 12 * rows * width)

    def swap(x, k):
        return lax.ppermute(x, AXIS, [(i, i ^ k) for i in range(n)])

    def cross(groups, *text_out):
        return pl.pallas_call(
            partial(cross_kernel, groups),
            out_shape=(bf16(rows, width),) + text_out,
            in_specs=[SMEM] + [VMEM] * 4,
            out_specs=(VMEM,) * (1 + len(text_out)),
            cost_estimate=big,
            compiler_params=PARAMS,
            name="cross",
        )(*cross_args)

    cross_args = (text_len, cq.reshape(rows, width), cc.reshape(rows, width), text_k, text_v)

    def temporal(messages, each):
        count = len(messages)
        return pl.pallas_call(
            partial(temporal_kernel, count, lanes),
            out_shape=tuple(bf16(3, each, width) for _ in messages),
            in_specs=[VMEM] * count,
            out_specs=(VMEM,) * count,
            cost_estimate=big,
            compiler_params=PARAMS,
            name="temporal",
        )(*messages)

    if not direct:
        packed = jnp.stack(flat).reshape(4, frames, n, lanes, width).transpose(2, 0, 1, 3, 4)
        moved = lax.all_to_all(packed, AXIS, 0, 0, tiled=True)
        moved = moved.transpose(1, 0, 2, 3, 4).reshape(4, rows, width)
        tiles = 2 * width // LANES
        grad_cross, partials = cross(1, f32(1, tiles * text, LANES))
        partials = partials.reshape(tiles, text, LANES).transpose(1, 0, 2).reshape(text, -1)
        text_grad = lax.psum_scatter(partials, AXIS, scatter_dimension=1, tiled=True)
        (back,) = temporal([moved], rows)
        back = back.reshape(3, n, frames, lanes, width).transpose(1, 0, 2, 3, 4)
        back = lax.all_to_all(back, AXIS, 0, 0, tiled=True)
        back = back.transpose(1, 2, 0, 3, 4).reshape(3, frames, positions, width)
        return back[0], back[1], back[2], grad_cross.reshape(cq.shape), text_grad

    each = positions // n
    messages = pl.pallas_call(
        partial(pack_kernel, n),
        out_shape=tuple(bf16(4, each, width) for _ in range(n)),
        in_specs=[HBM] * 4,
        out_specs=(VMEM,) * n,
        scratch_shapes=[pltpu.SemaphoreType.DMA((n, 4))],
        cost_estimate=cost(0, 16 * rows * width),
        compiler_params=PARAMS,
        name="pack",
    )(*[pltpu.with_memory_space_constraint(x, pltpu.HBM) for x in flat])
    messages, cross_args = lax.optimization_barrier((messages, cross_args))
    order = sorted(range(1, n), key=lambda k: (-(k.bit_length()), k))
    came = {0: messages[0]}
    for k in order:
        came[k] = swap(messages[k], k)

    high = text * columns // LANES
    grad_cross, stay, send = cross(n, f32(n // 2, high, LANES), bf16(n // 2, high, LANES))
    step = 1
    while True:
        got = swap(send, step)
        step *= 2
        if step == n:
            break
        both = stay + got.astype(jnp.float32)
        both = both.reshape(-1, 2, high, LANES)
        stay, send = both[:, 0], both[:, 1].astype(jnp.bfloat16)

    back = temporal([came[k] for k in range(n)], each)
    home = {0: back[0]}
    for k in order:
        home[k] = swap(back[k], k)
    out = pl.pallas_call(
        partial(unpack_kernel, n),
        out_shape=(bf16(rows, width),) * 3 + (f32(text, columns),),
        in_specs=[VMEM] * (n + 2),
        out_specs=(VMEM,) * 4,
        cost_estimate=cost(0, 12 * rows * width),
        compiler_params=PARAMS,
        name="unpack",
    )(*[home[k] for k in range(n)], stay, got)
    return tuple(x.reshape(tq.shape) for x in out[:3]) + (grad_cross.reshape(cq.shape), out[3])


def solution(mesh):
    n = mesh.shape[AXIS]
    token = P(("clip", "seq"), None, None)

    def body(*args):
        return local(n, *args)

    step = jax.shard_map(
        body,
        mesh=mesh,
        in_specs=(token,) * 6 + (P("clip", None), P("clip", None), P("clip")),
        out_specs=(token,) * 4 + (P("clip", "seq"),),
        check_vma=False,
    )
    return step if 4 <= n <= MOST_DIRECT else step
```

time: 82.7 us -> 73.5 us (0.89)
  Pallas kernels: 16 us -> 6.87 us
    pallas_call x2, Pallas kernels: 10.1 us -> 3.84 us  [the longest x1 2.82 us: cross(): pl.pallas_call(partial(cross_kernel, groups), out_shape=(bf16(rows, width...]
    pallas_call x1, Pallas kernels: 4.39 us -> 1.45 us  [temporal(): pl.pallas_call(partial(temporal_kernel, count, lanes), out_shape=tuple((b...]
  transfers between devices with their start and end apart: 17 -> 17, of which waited for: 6 -> 6; matrix products, arithmetic and copies ran while one was open for 0% -> 0% of each run, Pallas kernels for 5% -> 2%
where the time goes in v1:
time: 73.5 us; the launch traced here: 73.3 us
  starting transfers between devices  34.5 us (47%)
  waiting for transfers between devices  29.4 us (40%)
  Pallas kernels  6.87 us (9%)
  between operations  1.43 us (2%)
  local copies, waits for them, and re-layouts  1.02 us (1%)
    ppermute x17, starting transfers between devices, swap(): return lax.ppermute(x, AXIS, [(i, i ^ k) for i in range(n)])  34.5 us
    ppermute x17, waiting for transfers between devices, swap(): return lax.ppermute(x, AXIS, [(i, i ^ k) for i in range(n)])  29.4 us
    pallas_call x1, Pallas kernels, cross(): pl.pallas_call(partial(cross_kernel, groups), out_shape=(bf16(rows, width...  2.82 us
    pallas_call x1, Pallas kernels, local(): pl.pallas_call(partial(pack_kernel, n), out_shape=tuple((bf16(4, each, wi...  1.58 us
  transfers between devices with their start and end apart: 17, of which 6 were waited for; matrix products, arithmetic and copies ran while one was open for 0% of the time, Pallas kernels for 2%

profile of v1, /device:TPU:0, one launch (start us, length us, event | category | flops | bytes accessed | tf_op | source)
XLA Modules:
  0.0 73.3 jit_solution(18213927205500010181)
XLA Ops:
  1.3 0.0 copy-start
  1.3 0.0 copy-start.1
  1.3 0.0 copy-start.2
  1.3 1.6 %pack.1 = (bf16[4,16,1152]{2,1,0:T(8,128)(2,1)S(1)}, bf16[4,16,1152]{2,1,0:T(8,128)(2,1)S(1)}, bf16[4,16,1152]{2,1,0:T(8,128)(2,1)S(1)}, bf16[4,16,1152]{2,1,0:T...) custom-call(bf16[128,1152]{1,0:T(8,128)(2,1)} %bitcast.29, ...), custom_call_target="tpu_custom_call" | custom-call | bytes 2359296 | tf_op jit(solution)/shard_map/pack/pallas_call | solution.py:301
  2.9 0.0 copy-done
  2.9 0.0 copy-done.1
  2.9 0.0 copy-done.2
  2.9 0.0 copy-start.3
  2.9 1.0 %copy-done.3 = bf16[1,128,1152]{2,1,0:T(8,128)(2,1)S(1)} copy-done((bf16[1,128,1152]{2,1,0:T(8,128)(2,1)S(1)}, bf16[1,128,1152]{2,1,0:T(8,128)(2,1)}, u32[]{:S(2)}) %copy-start.3) | copy-done | bytes 294936
  3.9 2.8 %cross.1 = (bf16[128,1152]{1,0:T(8,128)(2,1)}, f32[4,360,128]{2,1,0:T(8,128)S(1)}, bf16[4,360,128]{2,1,0:T(8,128)(2,1)S(1)}) custom-call(s32[1]{0:T(128)S(6)} %copy.26.len_ref, bf16[128,1152]{1,0:T(8,128)(2,1)S(1)} %bitcast.25, bf16[128,1152]{1,0:T(8,128)(2,1)S(1)} %bitcast.26, bf16[160,1152]{1,0:T(8,128)(2,1)S(1)} %copy-done, bf16[160,1152]{1,0:T(8,128)(2,1)S(1)} %copy-done.1), custom_call_target="tpu_custom_call" | custom-call | flops 943718400 | bytes 1769472 | tf_op jit(solution)/shard_map/cross/pallas_call | solution.py:262
  6.7 3.0 %collective-permute-start.14 = (bf16[4,360,128]{2,1,0:T(8,128)(2,1)S(1)}, bf16[4,360,128]{2,1,0:T(8,128)(2,1)S(1)}, u32[]{:S(2)}, u32[]{:S(2)}) collective-permute-start(bf16[4,360,128]{2,1,0:T(8,128)(2,1)S(1)} %get-tuple-element.71), channel_id=1, source_target_pairs={{0,1},{1,0},{2,3},{3,2},{4,5},{5,4},{6,7},{7,6},{8,9},{9,8},{10,11... | collective-permute-start | bytes 1105928 | tf_op jit(solution)/shard_map/ppermute | solution.py:259
  9.7 0.0 collective-permute-start
  9.7 2.1 %collective-permute-start.1 = (bf16[4,16,1152]{2,1,0:T(8,128)(2,1)S(1)}, bf16[4,16,1152]{2,1,0:T(8,128)(2,1)S(1)}, u32[]{:S(2)}, u32[]{:S(2)}) collective-permute-start(bf16[4,16,1152]{2,1,0:T(8,128)(2,1)S(1)} %get-tuple-element.51), channel_id=1, source_target_pairs={{0,2},{1,3},{2,0},{3,1},{4,6},{5,7},{6,4},{7,5},{8,10},{9,11},{10,... | collective-permute-start | bytes 442376 | tf_op jit(solution)/shard_map/ppermute | solution.py:259
  11.8 1.4 %collective-permute-start.2 = (bf16[4,16,1152]{2,1,0:T(8,128)(2,1)S(1)}, bf16[4,16,1152]{2,1,0:T(8,128)(2,1)S(1)}, u32[]{:S(2)}, u32[]{:S(2)}) collective-permute-start(bf16[4,16,1152]{2,1,0:T(8,128)(2,1)S(1)} %get-tuple-element.52), channel_id=1, source_target_pairs={{0,3},{1,2},{2,1},{3,0},{4,7},{5,6},{6,5},{7,4},{8,11},{9,10},{10,... | collective-permute-start | bytes 442376 | tf_op jit(solution)/shard_map/ppermute | solution.py:259
  13.2 2.6 %collective-permute-start.3 = (bf16[4,16,1152]{2,1,0:T(8,128)(2,1)S(1)}, bf16[4,16,1152]{2,1,0:T(8,128)(2,1)S(1)}, u32[]{:S(2)}, u32[]{:S(2)}) collective-permute-start(bf16[4,16,1152]{2,1,0:T(8,128)(2,1)S(1)} %get-tuple-element.53), channel_id=1, source_target_pairs={{0,4},{1,5},{2,6},{3,7},{4,0},{5,1},{6,2},{7,3},{8,12},{9,13},{10,... | collective-permute-start | bytes 442376 | tf_op jit(solution)/shard_map/ppermute | solution.py:259
  15.8 6.1 %collective-permute-done.14 = bf16[4,360,128]{2,1,0:T(8,128)(2,1)S(1)} collective-permute-done((bf16[4,360,128]{2,1,0:T(8,128)(2,1)S(1)}, bf16[4,360,128]{2,1,0:T(8,128)(2,1)S(1)}, u32[]{:S(2)}, u32[]{:S(2)}) %collective-permute-start.14) | collective-permute-done | bytes 368672 | tf_op jit(solution)/shard_map/ppermute | solution.py:259
  21.8 4.5 %collective-permute-start.4 = (bf16[4,16,1152]{2,1,0:T(8,128)(2,1)S(1)}, bf16[4,16,1152]{2,1,0:T(8,128)(2,1)S(1)}, u32[]{:S(2)}, u32[]{:S(2)}) collective-permute-start(bf16[4,16,1152]{2,1,0:T(8,128)(2,1)S(1)} %get-tuple-element.54), channel_id=1, source_target_pairs={{0,5},{1,4},{2,7},{3,6},{4,1},{5,0},{6,3},{7,2},{8,13},{9,12},{10,... | collective-permute-start | bytes 442376 | tf_op jit(solution)/shard_map/ppermute | solution.py:259
  26.3 0.1 convert_add_fusion
  26.4 0.0 collective-permute-done.refs_1_
  26.4 3.6 %collective-permute-start.5 = (bf16[4,16,1152]{2,1,0:T(8,128)(2,1)S(1)}, bf16[4,16,1152]{2,1,0:T(8,128)(2,1)S(1)}, u32[]{:S(2)}, u32[]{:S(2)}) collective-permute-start(bf16[4,16,1152]{2,1,0:T(8,128)(2,1)S(1)} %get-tuple-element.55), channel_id=1, source_target_pairs={{0,6},{1,7},{2,4},{3,5},{4,2},{5,3},{6,0},{7,1},{8,14},{9,15},{10,... | collective-permute-start | bytes 442376 | tf_op jit(solution)/shard_map/ppermute | solution.py:259
  30.0 0.0 collective-permute-done.1.refs_2_
  30.0 1.1 %collective-permute-start.6 = (bf16[4,16,1152]{2,1,0:T(8,128)(2,1)S(1)}, bf16[4,16,1152]{2,1,0:T(8,128)(2,1)S(1)}, u32[]{:S(2)}, u32[]{:S(2)}) collective-permute-start(bf16[4,16,1152]{2,1,0:T(8,128)(2,1)S(1)} %get-tuple-element.56), channel_id=1, source_target_pairs={{0,7},{1,6},{2,5},{3,4},{4,3},{5,2},{6,1},{7,0},{8,15},{9,14},{10,... | collective-permute-start | bytes 442376 | tf_op jit(solution)/shard_map/ppermute | solution.py:259
  31.2 0.0 collective-permute-done.2.refs_3_
  31.2 0.1 collective-permute-start.15
  31.3 0.0 collective-permute-done.3.refs_4_
  31.3 7.1 %collective-permute-done.4.refs_5_ = bf16[4,16,1152]{2,1,0:T(8,128)(2,1)S(1)} collective-permute-done((bf16[4,16,1152]{2,1,0:T(8,128)(2,1)S(1)}, bf16[4,16,1152]{2,1,0:T(8,128)(2,1)S(1)}, u32[]{:S(2)}, u32[]{:S(2)}) %collective-permute-start.4) | collective-permute-done | bytes 147488 | tf_op jit(solution)/shard_map/ppermute | solution.py:259
  38.4 0.0 collective-permute-done.5.refs_6_
  38.4 1.0 %collective-permute-done.6.refs_7_ = bf16[4,16,1152]{2,1,0:T(8,128)(2,1)S(1)} collective-permute-done((bf16[4,16,1152]{2,1,0:T(8,128)(2,1)S(1)}, bf16[4,16,1152]{2,1,0:T(8,128)(2,1)S(1)}, u32[]{:S(2)}, u32[]{:S(2)}) %collective-permute-start.6) | collective-permute-done | bytes 147488 | tf_op jit(solution)/shard_map/ppermute | solution.py:259
  39.4 1.4 %temporal.1 = (bf16[3,16,1152]{2,1,0:T(8,128)(2,1)S(1)}, bf16[3,16,1152]{2,1,0:T(8,128)(2,1)S(1)}, bf16[3,16,1152]{2,1,0:T(8,128)(2,1)S(1)}, bf16[3,16,1152]{2,1...) custom-call(bf16[4,16,1152]{2,1,0:T(8,128)(2,1)S(1)} %get-tuple-elem, ...), custom_call_target="tpu_custom_call" | custom-call | flops 943718400 | bytes 1769472 | tf_op jit(solution)/shard_map/temporal/pallas_call | solution.py:276
  40.9 1.4 %collective-permute-start.7 = (bf16[3,16,1152]{2,1,0:T(8,128)(2,1)S(1)}, bf16[3,16,1152]{2,1,0:T(8,128)(2,1)S(1)}, u32[]{:S(2)}, u32[]{:S(2)}) collective-permute-start(bf16[3,16,1152]{2,1,0:T(8,128)(2,1)S(1)} %get-tuple-element.58), channel_id=1, source_target_pairs={{0,1},{1,0},{2,3},{3,2},{4,5},{5,4},{6,7},{7,6},{8,9},{9,8},{10,11... | collective-permute-start | bytes 331784 | tf_op jit(solution)/shard_map/ppermute | solution.py:259
  42.3 4.8 %collective-permute-start.8 = (bf16[3,16,1152]{2,1,0:T(8,128)(2,1)S(1)}, bf16[3,16,1152]{2,1,0:T(8,128)(2,1)S(1)}, u32[]{:S(2)}, u32[]{:S(2)}) collective-permute-start(bf16[3,16,1152]{2,1,0:T(8,128)(2,1)S(1)} %get-tuple-element.59), channel_id=1, source_target_pairs={{0,2},{1,3},{2,0},{3,1},{4,6},{5,7},{6,4},{7,5},{8,10},{9,11},{10,... | collective-permute-start | bytes 331784 | tf_op jit(solution)/shard_map/ppermute | solution.py:259
  47.1 0.5 collective-permute-start.9
  47.5 3.2 %collective-permute-start.10 = (bf16[3,16,1152]{2,1,0:T(8,128)(2,1)S(1)}, bf16[3,16,1152]{2,1,0:T(8,128)(2,1)S(1)}, u32[]{:S(2)}, u32[]{:S(2)}) collective-permute-start(bf16[3,16,1152]{2,1,0:T(8,128)(2,1)S(1)} %get-tuple-element.61), channel_id=1, source_target_pairs={{0,4},{1,5},{2,6},{3,7},{4,0},{5,1},{6,2},{7,3},{8,12},{9,13},{10,... | collective-permute-start | bytes 331784 | tf_op jit(solution)/shard_map/ppermute | solution.py:259
  50.8 0.0 collective-permute-done.15
  50.8 0.3 collective-permute-start.11
  51.2 0.0 collective-permute-done.7.refs_1_
  51.2 2.4 %collective-permute-start.12 = (bf16[3,16,1152]{2,1,0:T(8,128)(2,1)S(1)}, bf16[3,16,1152]{2,1,0:T(8,128)(2,1)S(1)}, u32[]{:S(2)}, u32[]{:S(2)}) collective-permute-start(bf16[3,16,1152]{2,1,0:T(8,128)(2,1)S(1)} %get-tuple-element.63), channel_id=1, source_target_pairs={{0,6},{1,7},{2,4},{3,5},{4,2},{5,3},{6,0},{7,1},{8,14},{9,15},{10,... | collective-permute-start | bytes 331784 | tf_op jit(solution)/shard_map/ppermute | solution.py:259
  53.6 0.0 collective-permute-done.8.refs_2_
  53.6 2.0 %collective-permute-start.13 = (bf16[3,16,1152]{2,1,0:T(8,128)(2,1)S(1)}, bf16[3,16,1152]{2,1,0:T(8,128)(2,1)S(1)}, u32[]{:S(2)}, u32[]{:S(2)}) collective-permute-start(bf16[3,16,1152]{2,1,0:T(8,128)(2,1)S(1)} %get-tuple-element.64), channel_id=1, source_target_pairs={{0,7},{1,6},{2,5},{3,4},{4,3},{5,2},{6,1},{7,0},{8,15},{9,14},{10,... | collective-permute-start | bytes 331784 | tf_op jit(solution)/shard_map/ppermute | solution.py:259
  55.6 0.0 collective-permute-done.9.refs_3_
  55.6 1.4 %collective-permute-start.16 = (bf16[1,360,128]{2,1,0:T(8,128)(2,1)S(1)}, bf16[1,360,128]{2,1,0:T(8,128)(2,1)S(1)}, u32[]{:S(2)}, u32[]{:S(2)}) collective-permute-start(bf16[1,360,128]{2,1,0:T(8,128)(2,1)S(1)} %fusion.3), channel_id=1, source_target_pairs={{0,4},{1,5},{2,6},{3,7},{4,0},{5,1},{6,2},{7,3},{8,12},{9,13},{10,... | collective-permute-start | bytes 276488 | tf_op jit(solution)/shard_map/ppermute | solution.py:259
  57.1 7.8 %collective-permute-done.10.refs_4_ = bf16[3,16,1152]{2,1,0:T(8,128)(2,1)S(1)} collective-permute-done((bf16[3,16,1152]{2,1,0:T(8,128)(2,1)S(1)}, bf16[3,16,1152]{2,1,0:T(8,128)(2,1)S(1)}, u32[]{:S(2)}, u32[]{:S(2)}) %collective-permute-start.10) | collective-permute-done | bytes 110624 | tf_op jit(solution)/shard_map/ppermute | solution.py:259
  64.9 2.1 %collective-permute-done.11.refs_5_ = bf16[3,16,1152]{2,1,0:T(8,128)(2,1)S(1)} collective-permute-done((bf16[3,16,1152]{2,1,0:T(8,128)(2,1)S(1)}, bf16[3,16,1152]{2,1,0:T(8,128)(2,1)S(1)}, u32[]{:S(2)}, u32[]{:S(2)}) %collective-permute-start.11) | collective-permute-done | bytes 110624 | tf_op jit(solution)/shard_map/ppermute | solution.py:259
  67.0 0.0 collective-permute-done.12.refs_6_
  67.0 0.0 collective-permute-done.13.refs_7_
  67.0 5.3 %collective-permute-done.16.refs_9_ = bf16[1,360,128]{2,1,0:T(8,128)(2,1)S(1)} collective-permute-done((bf16[1,360,128]{2,1,0:T(8,128)(2,1)S(1)}, bf16[1,360,128]{2,1,0:T(8,128)(2,1)S(1)}, u32[]{:S(2)}, u32[]{:S(2)}) %collective-permute-start.16) | collective-permute-done | bytes 92192 | tf_op jit(solution)/shard_map/ppermute | solution.py:259
  72.3 1.0 %unpack.1 = (bf16[128,1152]{1,0:T(8,128)(2,1)}, bf16[128,1152]{1,0:T(8,128)(2,1)}, bf16[128,1152]{1,0:T(8,128)(2,1)}, f32[160,288]{1,0:T(8,128)}) custom-call(bf16[3,16,1152]{2,1,0:T(8,128)(2,1)S(1)} %get-tuple-element.57.refs_0_, bf16[3,16,1152]{2,1,0:T(8,128)(2,1)S(1)} %collective-permute-done.7.refs_1_, ...), custom_call_target="tpu_custom_call" | custom-call | bytes 1769472 | tf_op jit(solution)/shard_map/unpack/pallas_call | solution.py:333
  (4 shorter events, 0.1 us)
Async XLA Ops:
  1.3 1.6 %copy-start = (bf16[160,1152]{1,0:T(8,128)(2,1)S(1)}, bf16[160,1152]{1,0:T(8,128)(2,1)}, u32[]{:S(2)}) copy-start(bf16[160,1152]{1,0:T(8,128)(2,1)} %k_ref) | copy-start | bytes 1105924
  1.3 1.6 %copy-start.1 = (bf16[160,1152]{1,0:T(8,128)(2,1)S(1)}, bf16[160,1152]{1,0:T(8,128)(2,1)}, u32[]{:S(2)}) copy-start(bf16[160,1152]{1,0:T(8,128)(2,1)} %v_ref) | copy-start | bytes 1105924
  1.3 1.6 %copy-start.2 = (bf16[1,128,1152]{2,1,0:T(8,128)(2,1)S(1)}, bf16[1,128,1152]{2,1,0:T(8,128)(2,1)}, u32[]{:S(2)}) copy-start(bf16[1,128,1152]{2,1,0:T(8,128)(2,1)} %param.13) | copy-start | bytes 884740
  2.9 1.0 %copy-start.3 = (bf16[1,128,1152]{2,1,0:T(8,128)(2,1)S(1)}, bf16[1,128,1152]{2,1,0:T(8,128)(2,1)}, u32[]{:S(2)}) copy-start(bf16[1,128,1152]{2,1,0:T(8,128)(2,1)} %param.14) | copy-start | bytes 884740
  6.7 15.1 %collective-permute-start.14 = (bf16[4,360,128]{2,1,0:T(8,128)(2,1)S(1)}, bf16[4,360,128]{2,1,0:T(8,128)(2,1)S(1)}, u32[]{:S(2)}, u32[]{:S(2)}) collective-permute-start(bf16[4,360,128]{2,1,0:T(8,128)(2,1)S(1)} %get-tuple-element.71), channel_id=1, source_target_pairs={{0,1},{1,0},{2,3},{3,2},{4,5},{5,4},{6,7},{7,6},{8,9},{9,8},{10,11... | collective-permute-start | bytes 1105928 | tf_op jit(solution)/shard_map/ppermute | solution.py:259
  9.7 16.7 %collective-permute-start = (bf16[4,16,1152]{2,1,0:T(8,128)(2,1)S(1)}, bf16[4,16,1152]{2,1,0:T(8,128)(2,1)S(1)}, u32[]{:S(2)}, u32[]{:S(2)}) collective-permute-start(bf16[4,16,1152]{2,1,0:T(8,128)(2,1)S(1)} %get-tuple-element.50), channel_id=1, source_target_pairs={{0,1},{1,0},{2,3},{3,2},{4,5},{5,4},{6,7},{7,6},{8,9},{9,8},{10,11... | collective-permute-start | bytes 442376 | tf_op jit(solution)/shard_map/ppermute | solution.py:259
  9.7 20.3 %collective-permute-start.1 = (bf16[4,16,1152]{2,1,0:T(8,128)(2,1)S(1)}, bf16[4,16,1152]{2,1,0:T(8,128)(2,1)S(1)}, u32[]{:S(2)}, u32[]{:S(2)}) collective-permute-start(bf16[4,16,1152]{2,1,0:T(8,128)(2,1)S(1)} %get-tuple-element.51), channel_id=1, source_target_pairs={{0,2},{1,3},{2,0},{3,1},{4,6},{5,7},{6,4},{7,5},{8,10},{9,11},{10,... | collective-permute-start | bytes 442376 | tf_op jit(solution)/shard_map/ppermute | solution.py:259
  11.8 19.4 %collective-permute-start.2 = (bf16[4,16,1152]{2,1,0:T(8,128)(2,1)S(1)}, bf16[4,16,1152]{2,1,0:T(8,128)(2,1)S(1)}, u32[]{:S(2)}, u32[]{:S(2)}) collective-permute-start(bf16[4,16,1152]{2,1,0:T(8,128)(2,1)S(1)} %get-tuple-element.52), channel_id=1, source_target_pairs={{0,3},{1,2},{2,1},{3,0},{4,7},{5,6},{6,5},{7,4},{8,11},{9,10},{10,... | collective-permute-start | bytes 442376 | tf_op jit(solution)/shard_map/ppermute | solution.py:259
  13.2 18.1 %collective-permute-start.3 = (bf16[4,16,1152]{2,1,0:T(8,128)(2,1)S(1)}, bf16[4,16,1152]{2,1,0:T(8,128)(2,1)S(1)}, u32[]{:S(2)}, u32[]{:S(2)}) collective-permute-start(bf16[4,16,1152]{2,1,0:T(8,128)(2,1)S(1)} %get-tuple-element.53), channel_id=1, source_target_pairs={{0,4},{1,5},{2,6},{3,7},{4,0},{5,1},{6,2},{7,3},{8,12},{9,13},{10,... | collective-permute-start | bytes 442376 | tf_op jit(solution)/shard_map/ppermute | solution.py:259
  21.8 16.6 %collective-permute-start.4 = (bf16[4,16,1152]{2,1,0:T(8,128)(2,1)S(1)}, bf16[4,16,1152]{2,1,0:T(8,128)(2,1)S(1)}, u32[]{:S(2)}, u32[]{:S(2)}) collective-permute-start(bf16[4,16,1152]{2,1,0:T(8,128)(2,1)S(1)} %get-tuple-element.54), channel_id=1, source_target_pairs={{0,5},{1,4},{2,7},{3,6},{4,1},{5,0},{6,3},{7,2},{8,13},{9,12},{10,... | collective-permute-start | bytes 442376 | tf_op jit(solution)/shard_map/ppermute | solution.py:259
  26.4 12.0 %collective-permute-start.5 = (bf16[4,16,1152]{2,1,0:T(8,128)(2,1)S(1)}, bf16[4,16,1152]{2,1,0:T(8,128)(2,1)S(1)}, u32[]{:S(2)}, u32[]{:S(2)}) collective-permute-start(bf16[4,16,1152]{2,1,0:T(8,128)(2,1)S(1)} %get-tuple-element.55), channel_id=1, source_target_pairs={{0,6},{1,7},{2,4},{3,5},{4,2},{5,3},{6,0},{7,1},{8,14},{9,15},{10,... | collective-permute-start | bytes 442376 | tf_op jit(solution)/shard_map/ppermute | solution.py:259
  30.0 9.4 %collective-permute-start.6 = (bf16[4,16,1152]{2,1,0:T(8,128)(2,1)S(1)}, bf16[4,16,1152]{2,1,0:T(8,128)(2,1)S(1)}, u32[]{:S(2)}, u32[]{:S(2)}) collective-permute-start(bf16[4,16,1152]{2,1,0:T(8,128)(2,1)S(1)} %get-tuple-element.56), channel_id=1, source_target_pairs={{0,7},{1,6},{2,5},{3,4},{4,3},{5,2},{6,1},{7,0},{8,15},{9,14},{10,... | collective-permute-start | bytes 442376 | tf_op jit(solution)/shard_map/ppermute | solution.py:259
  31.2 19.6 %collective-permute-start.15 = (bf16[2,360,128]{2,1,0:T(8,128)(2,1)S(1)}, bf16[2,360,128]{2,1,0:T(8,128)(2,1)S(1)}, u32[]{:S(2)}, u32[]{:S(2)}) collective-permute-start(bf16[2,360,128]{2,1,0:T(8,128)(2,1)S(1)} %fusion.2), channel_id=1, source_target_pairs={{0,2},{1,3},{2,0},{3,1},{4,6},{5,7},{6,4},{7,5},{8,10},{9,11},{10,... | collective-permute-start | bytes 552968 | tf_op jit(solution)/shard_map/ppermute | solution.py:259
  40.9 10.3 %collective-permute-start.7 = (bf16[3,16,1152]{2,1,0:T(8,128)(2,1)S(1)}, bf16[3,16,1152]{2,1,0:T(8,128)(2,1)S(1)}, u32[]{:S(2)}, u32[]{:S(2)}) collective-permute-start(bf16[3,16,1152]{2,1,0:T(8,128)(2,1)S(1)} %get-tuple-element.58), channel_id=1, source_target_pairs={{0,1},{1,0},{2,3},{3,2},{4,5},{5,4},{6,7},{7,6},{8,9},{9,8},{10,11... | collective-permute-start | bytes 331784 | tf_op jit(solution)/shard_map/ppermute | solution.py:259
  42.3 11.3 %collective-permute-start.8 = (bf16[3,16,1152]{2,1,0:T(8,128)(2,1)S(1)}, bf16[3,16,1152]{2,1,0:T(8,128)(2,1)S(1)}, u32[]{:S(2)}, u32[]{:S(2)}) collective-permute-start(bf16[3,16,1152]{2,1,0:T(8,128)(2,1)S(1)} %get-tuple-element.59), channel_id=1, source_target_pairs={{0,2},{1,3},{2,0},{3,1},{4,6},{5,7},{6,4},{7,5},{8,10},{9,11},{10,... | collective-permute-start | bytes 331784 | tf_op jit(solution)/shard_map/ppermute | solution.py:259
  47.1 8.6 %collective-permute-start.9 = (bf16[3,16,1152]{2,1,0:T(8,128)(2,1)S(1)}, bf16[3,16,1152]{2,1,0:T(8,128)(2,1)S(1)}, u32[]{:S(2)}, u32[]{:S(2)}) collective-permute-start(bf16[3,16,1152]{2,1,0:T(8,128)(2,1)S(1)} %get-tuple-element.60), channel_id=1, source_target_pairs={{0,3},{1,2},{2,1},{3,0},{4,7},{5,6},{6,5},{7,4},{8,11},{9,10},{10,... | collective-permute-start | bytes 331784 | tf_op jit(solution)/shard_map/ppermute | solution.py:259
  47.5 17.4 %collective-permute-start.10 = (bf16[3,16,1152]{2,1,0:T(8,128)(2,1)S(1)}, bf16[3,16,1152]{2,1,0:T(8,128)(2,1)S(1)}, u32[]{:S(2)}, u32[]{:S(2)}) collective-permute-start(bf16[3,16,1152]{2,1,0:T(8,128)(2,1)S(1)} %get-tuple-element.61), channel_id=1, source_target_pairs={{0,4},{1,5},{2,6},{3,7},{4,0},{5,1},{6,2},{7,3},{8,12},{9,13},{10,... | collective-permute-start | bytes 331784 | tf_op jit(solution)/shard_map/ppermute | solution.py:259
  50.8 16.2 %collective-permute-start.11 = (bf16[3,16,1152]{2,1,0:T(8,128)(2,1)S(1)}, bf16[3,16,1152]{2,1,0:T(8,128)(2,1)S(1)}, u32[]{:S(2)}, u32[]{:S(2)}) collective-permute-start(bf16[3,16,1152]{2,1,0:T(8,128)(2,1)S(1)} %get-tuple-element.62), channel_id=1, source_target_pairs={{0,5},{1,4},{2,7},{3,6},{4,1},{5,0},{6,3},{7,2},{8,13},{9,12},{10,... | collective-permute-start | bytes 331784 | tf_op jit(solution)/shard_map/ppermute | solution.py:259
  51.2 15.8 %collective-permute-start.12 = (bf16[3,16,1152]{2,1,0:T(8,128)(2,1)S(1)}, bf16[3,16,1152]{2,1,0:T(8,128)(2,1)S(1)}, u32[]{:S(2)}, u32[]{:S(2)}) collective-permute-start(bf16[3,16,1152]{2,1,0:T(8,128)(2,1)S(1)} %get-tuple-element.63), channel_id=1, source_target_pairs={{0,6},{1,7},{2,4},{3,5},{4,2},{5,3},{6,0},{7,1},{8,14},{9,15},{10,... | collective-permute-start | bytes 331784 | tf_op jit(solution)/shard_map/ppermute | solution.py:259
  53.6 13.4 %collective-permute-start.13 = (bf16[3,16,1152]{2,1,0:T(8,128)(2,1)S(1)}, bf16[3,16,1152]{2,1,0:T(8,128)(2,1)S(1)}, u32[]{:S(2)}, u32[]{:S(2)}) collective-permute-start(bf16[3,16,1152]{2,1,0:T(8,128)(2,1)S(1)} %get-tuple-element.64), channel_id=1, source_target_pairs={{0,7},{1,6},{2,5},{3,4},{4,3},{5,2},{6,1},{7,0},{8,15},{9,14},{10,... | collective-permute-start | bytes 331784 | tf_op jit(solution)/shard_map/ppermute | solution.py:259
  55.6 16.6 %collective-permute-start.16 = (bf16[1,360,128]{2,1,0:T(8,128)(2,1)S(1)}, bf16[1,360,128]{2,1,0:T(8,128)(2,1)S(1)}, u32[]{:S(2)}, u32[]{:S(2)}) collective-permute-start(bf16[1,360,128]{2,1,0:T(8,128)(2,1)S(1)} %fusion.3), channel_id=1, source_target_pairs={{0,4},{1,5},{2,6},{3,7},{4,0},{5,1},{6,2},{7,3},{8,12},{9,13},{10,... | collective-permute-start | bytes 276488 | tf_op jit(solution)/shard_map/ppermute | solution.py:259

commit v2 on v1

--- a/solution.py
+++ b/solution.py
@@ -12,6 +12,8 @@
 LANES = 128
 AXIS = "seq"
 MOST_DIRECT = 8
+
+CHUNKS = 2
 
 
 VMEM = pl.BlockSpec(memory_space=pltpu.VMEM)
@@ -160,42 +162,55 @@
     attend_back(heads, q, k, v, c, keep, 6, each_head, each_tile)
 
 
-def temporal_kernel(slots, lanes, *refs):
-    ins, outs = refs[:slots], refs[slots:]
-    each, width = ins[0].shape[1:]
-    rows = each * slots
+def temporal_kernel(slots, chunk, part, period, *refs):
+    ins, outs = refs[:slots], refs[-slots:]
+    before = refs[slots:-slots]
+    width = ins[0].shape[2]
+    rows = part * slots
     heads = Heads(width)
     keep = (
-        lax.broadcasted_iota(jnp.int32, (rows, rows), 0) % lanes
-        == lax.broadcasted_iota(jnp.int32, (rows, rows), 1) % lanes
+        lax.broadcasted_iota(jnp.int32, (rows, rows), 0) % period
+        == lax.broadcasted_iota(jnp.int32, (rows, rows), 1) % period
     )
-    q, k, v, c = (below(ref[t] for ref in ins) for t in range(4))
+
+    def mine(ref):
+        return slice(None) if ref.shape[1] == part else slice(chunk * part, (chunk + 1) * part)
+
+    q, k, v, c = (below(ref[t, mine(ref)] for ref in ins) for t in range(4))
+
+    def product(left, right):
+        if rows % LANES == 0:
+            return dot(beside(left), below(right), 1, 0)
+        return sum(dot(x, y, 1, 0) for x, y in zip(left, right))
 
     def each_tile(t, parts):
         slopes = [s for _, _, s, _, _ in parts]
         grads = (
             dot(below(slopes), below(k for *_, k, _ in parts), 0, 0),
-            dot(beside(slopes), below(heads.only(q, g, t) for g, *_ in parts), 1, 0),
-            dot(beside(r for _, r, *_ in parts), below(c for *_, c in parts), 1, 0),
+            product(slopes, [heads.only(q, g, t) for g, *_ in parts]),
+            product([r for _, r, *_ in parts], [c for *_, c in parts]),
         )
         for x, grad in enumerate(grads):
             grad = grad.astype(jnp.bfloat16)
             for i, ref in enumerate(outs):
-                ref[x, :, t * LANES : (t + 1) * LANES] = grad[i * each : (i + 1) * each]
-
+                ref[x, mine(ref), t * LANES : (t + 1) * LANES] = grad[i * part : (i + 1) * part]
+
+    whole = [ref for ref in outs if ref.shape[1] > part]
+    for i, ref in enumerate(before):
+        j, place = divmod(i, len(whole))
+        whole[place][:, j * part : (j + 1) * part] = ref[...]
     attend_back(heads, q, k, v, c, keep, 8, lambda *_: None, each_tile)
 
 
-def pack_kernel(slots, *refs):
+def pack_kernel(each, plan, *refs):
     ins, outs, sems = refs[:4], refs[4:-1], refs[-1]
-    each = ins[0].shape[0] // slots
     me = lax.axis_index(AXIS)
     copies = []
-    for k, out in enumerate(outs):
-        start = pl.multiple_of((me ^ k) * each, each)
+    for i, ((k, first, rows), out) in enumerate(zip(plan, outs)):
+        start = pl.multiple_of((me ^ k) * each + first, 8)
         for t, ref in enumerate(ins):
             copies.append(
-                pltpu.make_async_copy(ref.at[pl.ds(start, each)], out.at[t], sems.at[k, t])
+                pltpu.make_async_copy(ref.at[pl.ds(start, rows)], out.at[t], sems.at[i, t])
             )
     for copy in copies:
         copy.start()
@@ -203,14 +218,14 @@
         copy.wait()
 
 
-def unpack_kernel(slots, *refs):
-    ins, (kept, got), outs = refs[:slots], refs[slots : slots + 2], refs[slots + 2 :]
-    each = outs[0].shape[0] // slots
+def unpack_kernel(each, plan, *refs):
+    count = len(plan)
+    ins, (kept, got), outs = refs[:count], refs[count : count + 2], refs[count + 2 :]
     me = lax.axis_index(AXIS)
-    for k, ref in enumerate(ins):
-        start = pl.multiple_of((me ^ k) * each, each)
+    for (k, first, rows), ref in zip(plan, ins):
+        start = pl.multiple_of((me ^ k) * each + first, 8)
         for t in range(3):
-            outs[t][pl.ds(start, each), :] = ref[t]
+            outs[t][pl.ds(start, rows), :] = ref[t]
     total = kept[0] + got[0].astype(jnp.float32)
     text, columns = outs[3].shape
     whole, rest = divmod(columns, LANES)
@@ -271,17 +286,16 @@
 
     cross_args = (text_len, cq.reshape(rows, width), cc.reshape(rows, width), text_k, text_v)
 
-    def temporal(messages, each):
+    def temporal(messages, chunk, part, period, before, heights):
         count = len(messages)
         return pl.pallas_call(
-            partial(temporal_kernel, count, lanes),
-            out_shape=tuple(bf16(3, each, width) for _ in messages),
-            in_specs=[VMEM] * count,
+            partial(temporal_kernel, count, chunk, part, period),
+            out_shape=tuple(bf16(3, height, width) for height in heights),
+            in_specs=[VMEM] * (count + len(before)),
             out_specs=(VMEM,) * count,
             cost_estimate=big,
             compiler_params=PARAMS,
-            name="temporal",
-        )(*messages)
+        )(*messages, *before)
 
     if not direct:
         packed = jnp.stack(flat).reshape(4, frames, n, lanes, width).transpose(2, 0, 1, 3, 4)
@@ -291,28 +305,36 @@
         grad_cross, partials = cross(1, f32(1, tiles * text, LANES))
         partials = partials.reshape(tiles, text, LANES).transpose(1, 0, 2).reshape(text, -1)
         text_grad = lax.psum_scatter(partials, AXIS, scatter_dimension=1, tiled=True)
-        (back,) = temporal([moved], rows)
+        (back,) = temporal([moved], 0, rows, lanes, [], [rows])
         back = back.reshape(3, n, frames, lanes, width).transpose(1, 0, 2, 3, 4)
         back = lax.all_to_all(back, AXIS, 0, 0, tiled=True)
         back = back.transpose(1, 2, 0, 3, 4).reshape(3, frames, positions, width)
         return back[0], back[1], back[2], grad_cross.reshape(cq.shape), text_grad
 
     each = positions // n
+    chunks = CHUNKS if each % (8 * CHUNKS) == 0 else 1
+    part = each // chunks
+    near, far = range(n // 2), range(n // 2, n)
+    plan = [(k, 0, each) for k in near] + [(k, c * part, part) for c in range(chunks) for k in far]
     messages = pl.pallas_call(
-        partial(pack_kernel, n),
-        out_shape=tuple(bf16(4, each, width) for _ in range(n)),
+        partial(pack_kernel, each, plan),
+        out_shape=tuple(bf16(4, height, width) for _, _, height in plan),
         in_specs=[HBM] * 4,
-        out_specs=(VMEM,) * n,
-        scratch_shapes=[pltpu.SemaphoreType.DMA((n, 4))],
+        out_specs=(VMEM,) * len(plan),
+        scratch_shapes=[pltpu.SemaphoreType.DMA((len(plan), 4))],
         cost_estimate=cost(0, 16 * rows * width),
         compiler_params=PARAMS,
         name="pack",
     )(*[pltpu.with_memory_space_constraint(x, pltpu.HBM) for x in flat])
     messages, cross_args = lax.optimization_barrier((messages, cross_args))
-    order = sorted(range(1, n), key=lambda k: (-(k.bit_length()), k))
-    came = {0: messages[0]}
-    for k in order:
-        came[k] = swap(messages[k], k)
+
+    def exchange(plan, messages):
+        moved = {}
+        for (k, first, _), message in zip(plan, messages):
+            moved[k, first // part] = swap(message, k) if k else message
+        return moved
+
+    came = exchange(plan, messages)
 
     high = text * columns // LANES
     grad_cross, stay, send = cross(n, f32(n // 2, high, LANES), bf16(n // 2, high, LANES))
@@ -326,19 +348,25 @@
         both = both.reshape(-1, 2, high, LANES)
         stay, send = both[:, 0], both[:, 1].astype(jnp.bfloat16)
 
-    back = temporal([came[k] for k in range(n)], each)
-    home = {0: back[0]}
-    for k in order:
-        home[k] = swap(back[k], k)
+    home, before = {}, []
+    for c in range(chunks):
+        last = c == chunks - 1
+        got_now = [came[k, 0] for k in near] + [came[k, c] for k in far]
+        heights = [each if last else part] * len(near) + [part] * len(far)
+        back = temporal(got_now, c, part, part, before if last else [], heights)
+        home |= exchange([(k, c * part, part) for k in far], back[len(near) :])
+        if last:
+            home |= exchange([(k, 0, each) for k in near], back[: len(near)])
+        before += back[: len(near)]
     out = pl.pallas_call(
-        partial(unpack_kernel, n),
+        partial(unpack_kernel, each, plan),
         out_shape=(bf16(rows, width),) * 3 + (f32(text, columns),),
-        in_specs=[VMEM] * (n + 2),
+        in_specs=[VMEM] * (len(plan) + 2),
         out_specs=(VMEM,) * 4,
         cost_estimate=cost(0, 12 * rows * width),
         compiler_params=PARAMS,
         name="unpack",
-    )(*[home[k] for k in range(n)], stay, got)
+    )(*[home[k, first // part] for k, first, _ in plan], stay, got)
     return tuple(x.reshape(tq.shape) for x in out[:3]) + (grad_cross.reshape(cq.shape), out[3])
 
 

time: 73.5 us -> 72.9 us (level)
  waiting for transfers between devices: 29.4 us -> 13.8 us
  starting transfers between devices: 34.5 us -> 48.8 us
    ppermute x17 -> x25, waiting for transfers between devices: 29.4 us -> 13.8 us  [swap(): return lax.ppermute(x, AXIS, [(i, i ^ k) for i in range(n)])]
    ppermute x17 -> x25, starting transfers between devices: 34.5 us -> 48.8 us  [swap(): return lax.ppermute(x, AXIS, [(i, i ^ k) for i in range(n)])]
    pallas_call x3 -> x4, Pallas kernels: 4.05 us -> 4.64 us  [the longest x2 1.91 us: temporal(): pl.pallas_call(partial(temporal_kernel, count, chunk, part, period), out_...]
  transfers between devices with their start and end apart: 17 -> 25, of which waited for: 6 -> 11; matrix products, arithmetic and copies ran while one was open for 0% -> 0% of each run, Pallas kernels for 2% -> 3%
where the time goes in v2:
time: 72.9 us; the launch traced here: 72.7 us
  starting transfers between devices  48.8 us (67%)
  waiting for transfers between devices  13.8 us (19%)
  Pallas kernels  7.45 us (10%)
  between operations  1.46 us (2%)
  local copies, waits for them, and re-layouts  1.02 us (1%)
    ppermute x25, starting transfers between devices, swap(): return lax.ppermute(x, AXIS, [(i, i ^ k) for i in range(n)])  48.8 us
    ppermute x25, waiting for transfers between devices, swap(): return lax.ppermute(x, AXIS, [(i, i ^ k) for i in range(n)])  13.8 us
    pallas_call x1, Pallas kernels, cross(): pl.pallas_call(partial(cross_kernel, groups), out_shape=(bf16(rows, width...  2.81 us
    pallas_call x2, Pallas kernels, temporal(): pl.pallas_call(partial(temporal_kernel, count, chunk, part, period), out_...  1.91 us
    pallas_call x1, Pallas kernels, local(): pl.pallas_call(partial(pack_kernel, each, plan), out_shape=tuple((bf16(4,...  1.71 us
  transfers between devices with their start and end apart: 25, of which 11 were waited for; matrix products, arithmetic and copies ran while one was open for 0% of the time, Pallas kernels for 3%

profile of v2, /device:TPU:0, one launch (start us, length us, event | category | flops | bytes accessed | tf_op | source)
XLA Modules:
  0.0 72.7 jit_solution(13660535554847060010)
XLA Ops:
  1.3 1.7 %pack.1 = (bf16[4,16,1152]{2,1,0:T(8,128)(2,1)S(1)}, bf16[4,16,1152]{2,1,0:T(8,128)(2,1)S(1)}, bf16[4,16,1152]{2,1,0:T(8,128)(2,1)S(1)}, bf16[4,16,1152]{2,1,0:T...) custom-call(bf16[128,1152]{1,0:T(8,128)(2,1)} %bitcast.29, ...), custom_call_target="tpu_custom_call" | custom-call | bytes 2359296 | tf_op jit(solution)/shard_map/pack/pallas_call | solution.py:319
  3.1 0.0 copy-start.3
  3.1 1.0 %copy-done.3 = bf16[1,128,1152]{2,1,0:T(8,128)(2,1)S(1)} copy-done((bf16[1,128,1152]{2,1,0:T(8,128)(2,1)S(1)}, bf16[1,128,1152]{2,1,0:T(8,128)(2,1)}, u32[]{:S(2)}) %copy-start.3) | copy-done | bytes 294936
  4.0 2.8 %cross.1 = (bf16[128,1152]{1,0:T(8,128)(2,1)}, f32[4,360,128]{2,1,0:T(8,128)S(1)}, bf16[4,360,128]{2,1,0:T(8,128)(2,1)S(1)}) custom-call(s32[1]{0:T(128)S(6)} %copy.26.len_ref, bf16[128,1152]{1,0:T(8,128)(2,1)S(1)} %bitcast.25, bf16[128,1152]{1,0:T(8,128)(2,1)S(1)} %bitcast.26, bf16[160,1152]{1,0:T(8,128)(2,1)S(1)} %copy-done, bf16[160,1152]{1,0:T(8,128)(2,1)S(1)} %copy-done.1), custom_call_target="tpu_custom_call" | custom-call | flops 943718400 | bytes 1769472 | tf_op jit(solution)/shard_map/cross/pallas_call | solution.py:277
  6.8 3.0 %collective-permute-start.22 = (bf16[4,360,128]{2,1,0:T(8,128)(2,1)S(1)}, bf16[4,360,128]{2,1,0:T(8,128)(2,1)S(1)}, u32[]{:S(2)}, u32[]{:S(2)}) collective-permute-start(bf16[4,360,128]{2,1,0:T(8,128)(2,1)S(1)} %get-tuple-element.103), channel_id=1, source_target_pairs={{0,1},{1,0},{2,3},{3,2},{4,5},{5,4},{6,7},{7,6},{8,9},{9,8},{10,11... | collective-permute-start | bytes 1105928 | tf_op jit(solution)/shard_map/ppermute | solution.py:274
  9.8 2.6 %collective-permute-start.7 = (bf16[4,8,1152]{2,1,0:T(8,128)(2,1)S(1)}, bf16[4,8,1152]{2,1,0:T(8,128)(2,1)S(1)}, u32[]{:S(2)}, u32[]{:S(2)}) collective-permute-start(bf16[4,8,1152]{2,1,0:T(8,128)(2,1)S(1)} %get-tuple-element.77), channel_id=1, source_target_pairs={{0,4},{1,5},{2,6},{3,7},{4,0},{5,1},{6,2},{7,3},{8,12},{9,13},{10,... | collective-permute-start | bytes 221192 | tf_op jit(solution)/shard_map/ppermute | solution.py:274
  12.4 0.0 collective-permute-start.8
  12.4 3.9 %collective-permute-start.9 = (bf16[4,8,1152]{2,1,0:T(8,128)(2,1)S(1)}, bf16[4,8,1152]{2,1,0:T(8,128)(2,1)S(1)}, u32[]{:S(2)}, u32[]{:S(2)}) collective-permute-start(bf16[4,8,1152]{2,1,0:T(8,128)(2,1)S(1)} %get-tuple-element.79), channel_id=1, source_target_pairs={{0,6},{1,7},{2,4},{3,5},{4,2},{5,3},{6,0},{7,1},{8,14},{9,15},{10,... | collective-permute-start | bytes 221192 | tf_op jit(solution)/shard_map/ppermute | solution.py:274
  16.3 1.2 %collective-permute-start.10 = (bf16[4,8,1152]{2,1,0:T(8,128)(2,1)S(1)}, bf16[4,8,1152]{2,1,0:T(8,128)(2,1)S(1)}, u32[]{:S(2)}, u32[]{:S(2)}) collective-permute-start(bf16[4,8,1152]{2,1,0:T(8,128)(2,1)S(1)} %get-tuple-element.80), channel_id=1, source_target_pairs={{0,7},{1,6},{2,5},{3,4},{4,3},{5,2},{6,1},{7,0},{8,15},{9,14},{10,... | collective-permute-start | bytes 221192 | tf_op jit(solution)/shard_map/ppermute | solution.py:274
  17.5 1.7 %collective-permute-done.22 = bf16[4,360,128]{2,1,0:T(8,128)(2,1)S(1)} collective-permute-done((bf16[4,360,128]{2,1,0:T(8,128)(2,1)S(1)}, bf16[4,360,128]{2,1,0:T(8,128)(2,1)S(1)}, u32[]{:S(2)}, u32[]{:S(2)}) %collective-permute-start.22) | collective-permute-done | bytes 368672 | tf_op jit(solution)/shard_map/ppermute | solution.py:274
  19.2 1.1 %collective-permute-start = (bf16[4,16,1152]{2,1,0:T(8,128)(2,1)S(1)}, bf16[4,16,1152]{2,1,0:T(8,128)(2,1)S(1)}, u32[]{:S(2)}, u32[]{:S(2)}) collective-permute-start(bf16[4,16,1152]{2,1,0:T(8,128)(2,1)S(1)} %get-tuple-element.70), channel_id=1, source_target_pairs={{0,1},{1,0},{2,3},{3,2},{4,5},{5,4},{6,7},{7,6},{8,9},{9,8},{10,11... | collective-permute-start | bytes 442376 | tf_op jit(solution)/shard_map/ppermute | solution.py:274
  20.3 0.1 convert_add_fusion
  20.4 0.0 collective-permute-done.7.refs_4_
  20.4 3.0 %collective-permute-start.1 = (bf16[4,16,1152]{2,1,0:T(8,128)(2,1)S(1)}, bf16[4,16,1152]{2,1,0:T(8,128)(2,1)S(1)}, u32[]{:S(2)}, u32[]{:S(2)}) collective-permute-start(bf16[4,16,1152]{2,1,0:T(8,128)(2,1)S(1)} %get-tuple-element.71), channel_id=1, source_target_pairs={{0,2},{1,3},{2,0},{3,1},{4,6},{5,7},{6,4},{7,5},{8,10},{9,11},{10,... | collective-permute-start | bytes 442376 | tf_op jit(solution)/shard_map/ppermute | solution.py:274
  23.4 0.1 collective-permute-done.8.refs_5_
  23.5 0.0 collective-permute-start.2
  23.6 0.0 collective-permute-done.9.refs_6_
  23.6 2.0 %collective-permute-start.23 = (bf16[2,360,128]{2,1,0:T(8,128)(2,1)S(1)}, bf16[2,360,128]{2,1,0:T(8,128)(2,1)S(1)}, u32[]{:S(2)}, u32[]{:S(2)}) collective-permute-start(bf16[2,360,128]{2,1,0:T(8,128)(2,1)S(1)} %fusion.2), channel_id=1, source_target_pairs={{0,2},{1,3},{2,0},{3,1},{4,6},{5,7},{6,4},{7,5},{8,10},{9,11},{10,... | collective-permute-start | bytes 552968 | tf_op jit(solution)/shard_map/ppermute | solution.py:274
  25.5 2.6 %collective-permute-start.3 = (bf16[4,8,1152]{2,1,0:T(8,128)(2,1)S(1)}, bf16[4,8,1152]{2,1,0:T(8,128)(2,1)S(1)}, u32[]{:S(2)}, u32[]{:S(2)}) collective-permute-start(bf16[4,8,1152]{2,1,0:T(8,128)(2,1)S(1)} %get-tuple-element.73), channel_id=1, source_target_pairs={{0,4},{1,5},{2,6},{3,7},{4,0},{5,1},{6,2},{7,3},{8,12},{9,13},{10,... | collective-permute-start | bytes 221192 | tf_op jit(solution)/shard_map/ppermute | solution.py:274
  28.2 0.0 collective-permute-done.refs_1_
  28.2 3.9 %collective-permute-start.4 = (bf16[4,8,1152]{2,1,0:T(8,128)(2,1)S(1)}, bf16[4,8,1152]{2,1,0:T(8,128)(2,1)S(1)}, u32[]{:S(2)}, u32[]{:S(2)}) collective-permute-start(bf16[4,8,1152]{2,1,0:T(8,128)(2,1)S(1)} %get-tuple-element.74), channel_id=1, source_target_pairs={{0,5},{1,4},{2,7},{3,6},{4,1},{5,0},{6,3},{7,2},{8,13},{9,12},{10,... | collective-permute-start | bytes 221192 | tf_op jit(solution)/shard_map/ppermute | solution.py:274
  32.0 0.9 %collective-permute-start.5 = (bf16[4,8,1152]{2,1,0:T(8,128)(2,1)S(1)}, bf16[4,8,1152]{2,1,0:T(8,128)(2,1)S(1)}, u32[]{:S(2)}, u32[]{:S(2)}) collective-permute-start(bf16[4,8,1152]{2,1,0:T(8,128)(2,1)S(1)} %get-tuple-element.75), channel_id=1, source_target_pairs={{0,6},{1,7},{2,4},{3,5},{4,2},{5,3},{6,0},{7,1},{8,14},{9,15},{10,... | collective-permute-start | bytes 221192 | tf_op jit(solution)/shard_map/ppermute | solution.py:274
  33.0 0.5 collective-permute-done.2.refs_3_
  33.5 6.1 %collective-permute-start.6 = (bf16[4,8,1152]{2,1,0:T(8,128)(2,1)S(1)}, bf16[4,8,1152]{2,1,0:T(8,128)(2,1)S(1)}, u32[]{:S(2)}, u32[]{:S(2)}) collective-permute-start(bf16[4,8,1152]{2,1,0:T(8,128)(2,1)S(1)} %get-tuple-element.76), channel_id=1, source_target_pairs={{0,7},{1,6},{2,5},{3,4},{4,3},{5,2},{6,1},{7,0},{8,15},{9,14},{10,... | collective-permute-start | bytes 221192 | tf_op jit(solution)/shard_map/ppermute | solution.py:274
  39.6 0.9 %shard_map.128 = (bf16[3,8,1152]{2,1,0:T(8,128)(2,1)S(1)}, bf16[3,8,1152]{2,1,0:T(8,128)(2,1)S(1)}, bf16[3,8,1152]{2,1,0:T(8,128)(2,1)S(1)}, bf16[3,8,1152]{2,1,...) custom-call(bf16[4,16,1152]{2,1,0:T(8,128)(2,1)S(1)} %get-tuple-elem, ...), custom_call_target="tpu_custom_call" | custom-call | flops 943718400 | bytes 1769472 | tf_op jit(solution)/shard_map/pallas_call | solution.py:291
  40.6 0.0 collective-permute-done.4.refs_5_
  40.6 0.5 collective-permute-done.5.refs_6_
  41.1 1.5 %collective-permute-done.6.refs_7_ = bf16[4,8,1152]{2,1,0:T(8,128)(2,1)S(1)} collective-permute-done((bf16[4,8,1152]{2,1,0:T(8,128)(2,1)S(1)}, bf16[4,8,1152]{2,1,0:T(8,128)(2,1)S(1)}, u32[]{:S(2)}, u32[]{:S(2)}) %collective-permute-start.6) | collective-permute-done | bytes 73760 | tf_op jit(solution)/shard_map/ppermute | solution.py:274
  42.5 1.0 %shard_map.129 = (bf16[3,16,1152]{2,1,0:T(8,128)(2,1)S(1)}, bf16[3,16,1152]{2,1,0:T(8,128)(2,1)S(1)}, bf16[3,16,1152]{2,1,0:T(8,128)(2,1)S(1)}, bf16[3,16,1152]{...) custom-call(bf16[4,16,1152]{2,1,0:T(8,128)(2,1)S(1)} %get-tuple-elem, ...), custom_call_target="tpu_custom_call" | custom-call | flops 943718400 | bytes 1769472 | tf_op jit(solution)/shard_map/pallas_call | solution.py:291
  43.5 1.4 %collective-permute-start.18 = (bf16[3,8,1152]{2,1,0:T(8,128)(2,1)S(1)}, bf16[3,8,1152]{2,1,0:T(8,128)(2,1)S(1)}, u32[]{:S(2)}, u32[]{:S(2)}) collective-permute-start(bf16[3,8,1152]{2,1,0:T(8,128)(2,1)S(1)} %get-tuple-element.93), channel_id=1, source_target_pairs={{0,4},{1,5},{2,6},{3,7},{4,0},{5,1},{6,2},{7,3},{8,12},{9,13},{10,... | collective-permute-start | bytes 165896 | tf_op jit(solution)/shard_map/ppermute | solution.py:274
  44.9 1.8 %collective-permute-start.19 = (bf16[3,8,1152]{2,1,0:T(8,128)(2,1)S(1)}, bf16[3,8,1152]{2,1,0:T(8,128)(2,1)S(1)}, u32[]{:S(2)}, u32[]{:S(2)}) collective-permute-start(bf16[3,8,1152]{2,1,0:T(8,128)(2,1)S(1)} %get-tuple-element.94), channel_id=1, source_target_pairs={{0,5},{1,4},{2,7},{3,6},{4,1},{5,0},{6,3},{7,2},{8,13},{9,12},{10,... | collective-permute-start | bytes 165896 | tf_op jit(solution)/shard_map/ppermute | solution.py:274
  46.7 3.9 %collective-permute-start.20 = (bf16[3,8,1152]{2,1,0:T(8,128)(2,1)S(1)}, bf16[3,8,1152]{2,1,0:T(8,128)(2,1)S(1)}, u32[]{:S(2)}, u32[]{:S(2)}) collective-permute-start(bf16[3,8,1152]{2,1,0:T(8,128)(2,1)S(1)} %get-tuple-element.95), channel_id=1, source_target_pairs={{0,6},{1,7},{2,4},{3,5},{4,2},{5,3},{6,0},{7,1},{8,14},{9,15},{10,... | collective-permute-start | bytes 165896 | tf_op jit(solution)/shard_map/ppermute | solution.py:274
  50.6 0.6 collective-permute-start.21
  51.2 0.0 collective-permute-done.23
  51.3 3.3 %collective-permute-start.15 = (bf16[3,8,1152]{2,1,0:T(8,128)(2,1)S(1)}, bf16[3,8,1152]{2,1,0:T(8,128)(2,1)S(1)}, u32[]{:S(2)}, u32[]{:S(2)}) collective-permute-start(bf16[3,8,1152]{2,1,0:T(8,128)(2,1)S(1)} %get-tuple-element.90), channel_id=1, source_target_pairs={{0,5},{1,4},{2,7},{3,6},{4,1},{5,0},{6,3},{7,2},{8,13},{9,12},{10,... | collective-permute-start | bytes 165896 | tf_op jit(solution)/shard_map/ppermute | solution.py:274
  54.5 1.3 %collective-permute-done.19.refs_9_ = bf16[3,8,1152]{2,1,0:T(8,128)(2,1)S(1)} collective-permute-done((bf16[3,8,1152]{2,1,0:T(8,128)(2,1)S(1)}, bf16[3,8,1152]{2,1,0:T(8,128)(2,1)S(1)}, u32[]{:S(2)}, u32[]{:S(2)}) %collective-permute-start.19) | collective-permute-done | bytes 55328 | tf_op jit(solution)/shard_map/ppermute | solution.py:274
  55.8 3.7 %collective-permute-start.16 = (bf16[3,8,1152]{2,1,0:T(8,128)(2,1)S(1)}, bf16[3,8,1152]{2,1,0:T(8,128)(2,1)S(1)}, u32[]{:S(2)}, u32[]{:S(2)}) collective-permute-start(bf16[3,8,1152]{2,1,0:T(8,128)(2,1)S(1)} %get-tuple-element.91), channel_id=1, source_target_pairs={{0,6},{1,7},{2,4},{3,5},{4,2},{5,3},{6,0},{7,1},{8,14},{9,15},{10,... | collective-permute-start | bytes 165896 | tf_op jit(solution)/shard_map/ppermute | solution.py:274
  59.6 0.1 collective-permute-start.17
  59.7 1.5 %collective-permute-start.11 = (bf16[3,16,1152]{2,1,0:T(8,128)(2,1)S(1)}, bf16[3,16,1152]{2,1,0:T(8,128)(2,1)S(1)}, u32[]{:S(2)}, u32[]{:S(2)}) collective-permute-start(bf16[3,16,1152]{2,1,0:T(8,128)(2,1)S(1)} %get-tuple-element.86), channel_id=1, source_target_pairs={{0,1},{1,0},{2,3},{3,2},{4,5},{5,4},{6,7},{7,6},{8,9},{9,8},{10,11... | collective-permute-start | bytes 331784 | tf_op jit(solution)/shard_map/ppermute | solution.py:274
  61.2 1.0 %collective-permute-done.14.refs_4_ = bf16[3,8,1152]{2,1,0:T(8,128)(2,1)S(1)} collective-permute-done((bf16[3,8,1152]{2,1,0:T(8,128)(2,1)S(1)}, bf16[3,8,1152]{2,1,0:T(8,128)(2,1)S(1)}, u32[]{:S(2)}, u32[]{:S(2)}) %collective-permute-start.14) | collective-permute-done | bytes 55328 | tf_op jit(solution)/shard_map/ppermute | solution.py:274
  62.2 0.1 collective-permute-start.12
  62.3 1.8 %collective-permute-done.15.refs_5_ = bf16[3,8,1152]{2,1,0:T(8,128)(2,1)S(1)} collective-permute-done((bf16[3,8,1152]{2,1,0:T(8,128)(2,1)S(1)}, bf16[3,8,1152]{2,1,0:T(8,128)(2,1)S(1)}, u32[]{:S(2)}, u32[]{:S(2)}) %collective-permute-start.15) | collective-permute-done | bytes 55328 | tf_op jit(solution)/shard_map/ppermute | solution.py:274
  64.1 0.8 %collective-permute-start.13 = (bf16[3,16,1152]{2,1,0:T(8,128)(2,1)S(1)}, bf16[3,16,1152]{2,1,0:T(8,128)(2,1)S(1)}, u32[]{:S(2)}, u32[]{:S(2)}) collective-permute-start(bf16[3,16,1152]{2,1,0:T(8,128)(2,1)S(1)} %get-tuple-element.88), channel_id=1, source_target_pairs={{0,3},{1,2},{2,1},{3,0},{4,7},{5,6},{6,5},{7,4},{8,11},{9,10},{10,... | collective-permute-start | bytes 331784 | tf_op jit(solution)/shard_map/ppermute | solution.py:274
  65.0 1.3 %collective-permute-start.24 = (bf16[1,360,128]{2,1,0:T(8,128)(2,1)S(1)}, bf16[1,360,128]{2,1,0:T(8,128)(2,1)S(1)}, u32[]{:S(2)}, u32[]{:S(2)}) collective-permute-start(bf16[1,360,128]{2,1,0:T(8,128)(2,1)S(1)} %fusion.3), channel_id=1, source_target_pairs={{0,4},{1,5},{2,6},{3,7},{4,0},{5,1},{6,2},{7,3},{8,12},{9,13},{10,... | collective-permute-start | bytes 276488 | tf_op jit(solution)/shard_map/ppermute | solution.py:274
  66.3 0.4 collective-permute-done.17.refs_7_
  66.7 1.3 %collective-permute-done.12.refs_2_ = bf16[3,16,1152]{2,1,0:T(8,128)(2,1)S(1)} collective-permute-done((bf16[3,16,1152]{2,1,0:T(8,128)(2,1)S(1)}, bf16[3,16,1152]{2,1,0:T(8,128)(2,1)S(1)}, u32[]{:S(2)}, u32[]{:S(2)}) %collective-permute-start.12) | collective-permute-done | bytes 110624 | tf_op jit(solution)/shard_map/ppermute | solution.py:274
  68.0 3.7 %collective-permute-done.13.refs_3_ = bf16[3,16,1152]{2,1,0:T(8,128)(2,1)S(1)} collective-permute-done((bf16[3,16,1152]{2,1,0:T(8,128)(2,1)S(1)}, bf16[3,16,1152]{2,1,0:T(8,128)(2,1)S(1)}, u32[]{:S(2)}, u32[]{:S(2)}) %collective-permute-start.13) | collective-permute-done | bytes 110624 | tf_op jit(solution)/shard_map/ppermute | solution.py:274
  71.7 1.0 %unpack.1 = (bf16[128,1152]{1,0:T(8,128)(2,1)}, bf16[128,1152]{1,0:T(8,128)(2,1)}, bf16[128,1152]{1,0:T(8,128)(2,1)}, f32[160,288]{1,0:T(8,128)}) custom-call(bf16[3,16,1152]{2,1,0:T(8,128)(2,1)S(1)} %get-tuple-element.85.refs_0_, bf16[3,16,1152]{2,1,0:T(8,128)(2,1)S(1)} %collective-permute-done.11.refs_1_, ...), custom_call_target="tpu_custom_call" | custom-call | bytes 1769472 | tf_op jit(solution)/shard_map/unpack/pallas_call | solution.py:361
  (20 shorter events, 0.1 us)
Async XLA Ops:
  1.3 1.8 %copy-start = (bf16[160,1152]{1,0:T(8,128)(2,1)S(1)}, bf16[160,1152]{1,0:T(8,128)(2,1)}, u32[]{:S(2)}) copy-start(bf16[160,1152]{1,0:T(8,128)(2,1)} %k_ref) | copy-start | bytes 1105924
  1.3 1.8 %copy-start.1 = (bf16[160,1152]{1,0:T(8,128)(2,1)S(1)}, bf16[160,1152]{1,0:T(8,128)(2,1)}, u32[]{:S(2)}) copy-start(bf16[160,1152]{1,0:T(8,128)(2,1)} %v_ref) | copy-start | bytes 1105924
  1.3 1.8 %copy-start.2 = (bf16[1,128,1152]{2,1,0:T(8,128)(2,1)S(1)}, bf16[1,128,1152]{2,1,0:T(8,128)(2,1)}, u32[]{:S(2)}) copy-start(bf16[1,128,1152]{2,1,0:T(8,128)(2,1)} %param.13) | copy-start | bytes 884740
  3.1 1.0 %copy-start.3 = (bf16[1,128,1152]{2,1,0:T(8,128)(2,1)S(1)}, bf16[1,128,1152]{2,1,0:T(8,128)(2,1)}, u32[]{:S(2)}) copy-start(bf16[1,128,1152]{2,1,0:T(8,128)(2,1)} %param.14) | copy-start | bytes 884740
  6.8 12.4 %collective-permute-start.22 = (bf16[4,360,128]{2,1,0:T(8,128)(2,1)S(1)}, bf16[4,360,128]{2,1,0:T(8,128)(2,1)S(1)}, u32[]{:S(2)}, u32[]{:S(2)}) collective-permute-start(bf16[4,360,128]{2,1,0:T(8,128)(2,1)S(1)} %get-tuple-element.103), channel_id=1, source_target_pairs={{0,1},{1,0},{2,3},{3,2},{4,5},{5,4},{6,7},{7,6},{8,9},{9,8},{10,11... | collective-permute-start | bytes 1105928 | tf_op jit(solution)/shard_map/ppermute | solution.py:274
  9.8 10.6 %collective-permute-start.7 = (bf16[4,8,1152]{2,1,0:T(8,128)(2,1)S(1)}, bf16[4,8,1152]{2,1,0:T(8,128)(2,1)S(1)}, u32[]{:S(2)}, u32[]{:S(2)}) collective-permute-start(bf16[4,8,1152]{2,1,0:T(8,128)(2,1)S(1)} %get-tuple-element.77), channel_id=1, source_target_pairs={{0,4},{1,5},{2,6},{3,7},{4,0},{5,1},{6,2},{7,3},{8,12},{9,13},{10,... | collective-permute-start | bytes 221192 | tf_op jit(solution)/shard_map/ppermute | solution.py:274
  12.4 11.1 %collective-permute-start.8 = (bf16[4,8,1152]{2,1,0:T(8,128)(2,1)S(1)}, bf16[4,8,1152]{2,1,0:T(8,128)(2,1)S(1)}, u32[]{:S(2)}, u32[]{:S(2)}) collective-permute-start(bf16[4,8,1152]{2,1,0:T(8,128)(2,1)S(1)} %get-tuple-element.78), channel_id=1, source_target_pairs={{0,5},{1,4},{2,7},{3,6},{4,1},{5,0},{6,3},{7,2},{8,13},{9,12},{10,... | collective-permute-start | bytes 221192 | tf_op jit(solution)/shard_map/ppermute | solution.py:274
  12.4 11.2 %collective-permute-start.9 = (bf16[4,8,1152]{2,1,0:T(8,128)(2,1)S(1)}, bf16[4,8,1152]{2,1,0:T(8,128)(2,1)S(1)}, u32[]{:S(2)}, u32[]{:S(2)}) collective-permute-start(bf16[4,8,1152]{2,1,0:T(8,128)(2,1)S(1)} %get-tuple-element.79), channel_id=1, source_target_pairs={{0,6},{1,7},{2,4},{3,5},{4,2},{5,3},{6,0},{7,1},{8,14},{9,15},{10,... | collective-permute-start | bytes 221192 | tf_op jit(solution)/shard_map/ppermute | solution.py:274
  16.3 9.2 %collective-permute-start.10 = (bf16[4,8,1152]{2,1,0:T(8,128)(2,1)S(1)}, bf16[4,8,1152]{2,1,0:T(8,128)(2,1)S(1)}, u32[]{:S(2)}, u32[]{:S(2)}) collective-permute-start(bf16[4,8,1152]{2,1,0:T(8,128)(2,1)S(1)} %get-tuple-element.80), channel_id=1, source_target_pairs={{0,7},{1,6},{2,5},{3,4},{4,3},{5,2},{6,1},{7,0},{8,15},{9,14},{10,... | collective-permute-start | bytes 221192 | tf_op jit(solution)/shard_map/ppermute | solution.py:274
  19.2 9.0 %collective-permute-start = (bf16[4,16,1152]{2,1,0:T(8,128)(2,1)S(1)}, bf16[4,16,1152]{2,1,0:T(8,128)(2,1)S(1)}, u32[]{:S(2)}, u32[]{:S(2)}) collective-permute-start(bf16[4,16,1152]{2,1,0:T(8,128)(2,1)S(1)} %get-tuple-element.70), channel_id=1, source_target_pairs={{0,1},{1,0},{2,3},{3,2},{4,5},{5,4},{6,7},{7,6},{8,9},{9,8},{10,11... | collective-permute-start | bytes 442376 | tf_op jit(solution)/shard_map/ppermute | solution.py:274
  20.4 11.7 %collective-permute-start.1 = (bf16[4,16,1152]{2,1,0:T(8,128)(2,1)S(1)}, bf16[4,16,1152]{2,1,0:T(8,128)(2,1)S(1)}, u32[]{:S(2)}, u32[]{:S(2)}) collective-permute-start(bf16[4,16,1152]{2,1,0:T(8,128)(2,1)S(1)} %get-tuple-element.71), channel_id=1, source_target_pairs={{0,2},{1,3},{2,0},{3,1},{4,6},{5,7},{6,4},{7,5},{8,10},{9,11},{10,... | collective-permute-start | bytes 442376 | tf_op jit(solution)/shard_map/ppermute | solution.py:274
  23.5 10.0 %collective-permute-start.2 = (bf16[4,16,1152]{2,1,0:T(8,128)(2,1)S(1)}, bf16[4,16,1152]{2,1,0:T(8,128)(2,1)S(1)}, u32[]{:S(2)}, u32[]{:S(2)}) collective-permute-start(bf16[4,16,1152]{2,1,0:T(8,128)(2,1)S(1)} %get-tuple-element.72), channel_id=1, source_target_pairs={{0,3},{1,2},{2,1},{3,0},{4,7},{5,6},{6,5},{7,4},{8,11},{9,10},{10,... | collective-permute-start | bytes 442376 | tf_op jit(solution)/shard_map/ppermute | solution.py:274
  23.6 27.6 %collective-permute-start.23 = (bf16[2,360,128]{2,1,0:T(8,128)(2,1)S(1)}, bf16[2,360,128]{2,1,0:T(8,128)(2,1)S(1)}, u32[]{:S(2)}, u32[]{:S(2)}) collective-permute-start(bf16[2,360,128]{2,1,0:T(8,128)(2,1)S(1)} %fusion.2), channel_id=1, source_target_pairs={{0,2},{1,3},{2,0},{3,1},{4,6},{5,7},{6,4},{7,5},{8,10},{9,11},{10,... | collective-permute-start | bytes 552968 | tf_op jit(solution)/shard_map/ppermute | solution.py:274
  25.5 15.0 %collective-permute-start.3 = (bf16[4,8,1152]{2,1,0:T(8,128)(2,1)S(1)}, bf16[4,8,1152]{2,1,0:T(8,128)(2,1)S(1)}, u32[]{:S(2)}, u32[]{:S(2)}) collective-permute-start(bf16[4,8,1152]{2,1,0:T(8,128)(2,1)S(1)} %get-tuple-element.73), channel_id=1, source_target_pairs={{0,4},{1,5},{2,6},{3,7},{4,0},{5,1},{6,2},{7,3},{8,12},{9,13},{10,... | collective-permute-start | bytes 221192 | tf_op jit(solution)/shard_map/ppermute | solution.py:274
  28.2 12.4 %collective-permute-start.4 = (bf16[4,8,1152]{2,1,0:T(8,128)(2,1)S(1)}, bf16[4,8,1152]{2,1,0:T(8,128)(2,1)S(1)}, u32[]{:S(2)}, u32[]{:S(2)}) collective-permute-start(bf16[4,8,1152]{2,1,0:T(8,128)(2,1)S(1)} %get-tuple-element.74), channel_id=1, source_target_pairs={{0,5},{1,4},{2,7},{3,6},{4,1},{5,0},{6,3},{7,2},{8,13},{9,12},{10,... | collective-permute-start | bytes 221192 | tf_op jit(solution)/shard_map/ppermute | solution.py:274
  32.0 9.0 %collective-permute-start.5 = (bf16[4,8,1152]{2,1,0:T(8,128)(2,1)S(1)}, bf16[4,8,1152]{2,1,0:T(8,128)(2,1)S(1)}, u32[]{:S(2)}, u32[]{:S(2)}) collective-permute-start(bf16[4,8,1152]{2,1,0:T(8,128)(2,1)S(1)} %get-tuple-element.75), channel_id=1, source_target_pairs={{0,6},{1,7},{2,4},{3,5},{4,2},{5,3},{6,0},{7,1},{8,14},{9,15},{10,... | collective-permute-start | bytes 221192 | tf_op jit(solution)/shard_map/ppermute | solution.py:274
  33.5 9.0 %collective-permute-start.6 = (bf16[4,8,1152]{2,1,0:T(8,128)(2,1)S(1)}, bf16[4,8,1152]{2,1,0:T(8,128)(2,1)S(1)}, u32[]{:S(2)}, u32[]{:S(2)}) collective-permute-start(bf16[4,8,1152]{2,1,0:T(8,128)(2,1)S(1)} %get-tuple-element.76), channel_id=1, source_target_pairs={{0,7},{1,6},{2,5},{3,4},{4,3},{5,2},{6,1},{7,0},{8,15},{9,14},{10,... | collective-permute-start | bytes 221192 | tf_op jit(solution)/shard_map/ppermute | solution.py:274
  43.5 7.8 %collective-permute-start.18 = (bf16[3,8,1152]{2,1,0:T(8,128)(2,1)S(1)}, bf16[3,8,1152]{2,1,0:T(8,128)(2,1)S(1)}, u32[]{:S(2)}, u32[]{:S(2)}) collective-permute-start(bf16[3,8,1152]{2,1,0:T(8,128)(2,1)S(1)} %get-tuple-element.93), channel_id=1, source_target_pairs={{0,4},{1,5},{2,6},{3,7},{4,0},{5,1},{6,2},{7,3},{8,12},{9,13},{10,... | collective-permute-start | bytes 165896 | tf_op jit(solution)/shard_map/ppermute | solution.py:274
  44.9 10.9 %collective-permute-start.19 = (bf16[3,8,1152]{2,1,0:T(8,128)(2,1)S(1)}, bf16[3,8,1152]{2,1,0:T(8,128)(2,1)S(1)}, u32[]{:S(2)}, u32[]{:S(2)}) collective-permute-start(bf16[3,8,1152]{2,1,0:T(8,128)(2,1)S(1)} %get-tuple-element.94), channel_id=1, source_target_pairs={{0,5},{1,4},{2,7},{3,6},{4,1},{5,0},{6,3},{7,2},{8,13},{9,12},{10,... | collective-permute-start | bytes 165896 | tf_op jit(solution)/shard_map/ppermute | solution.py:274
  46.7 12.9 %collective-permute-start.20 = (bf16[3,8,1152]{2,1,0:T(8,128)(2,1)S(1)}, bf16[3,8,1152]{2,1,0:T(8,128)(2,1)S(1)}, u32[]{:S(2)}, u32[]{:S(2)}) collective-permute-start(bf16[3,8,1152]{2,1,0:T(8,128)(2,1)S(1)} %get-tuple-element.95), channel_id=1, source_target_pairs={{0,6},{1,7},{2,4},{3,5},{4,2},{5,3},{6,0},{7,1},{8,14},{9,15},{10,... | collective-permute-start | bytes 165896 | tf_op jit(solution)/shard_map/ppermute | solution.py:274
  50.6 9.1 %collective-permute-start.21 = (bf16[3,8,1152]{2,1,0:T(8,128)(2,1)S(1)}, bf16[3,8,1152]{2,1,0:T(8,128)(2,1)S(1)}, u32[]{:S(2)}, u32[]{:S(2)}) collective-permute-start(bf16[3,8,1152]{2,1,0:T(8,128)(2,1)S(1)} %get-tuple-element.96), channel_id=1, source_target_pairs={{0,7},{1,6},{2,5},{3,4},{4,3},{5,2},{6,1},{7,0},{8,15},{9,14},{10,... | collective-permute-start | bytes 165896 | tf_op jit(solution)/shard_map/ppermute | solution.py:274
  51.2 11.0 %collective-permute-start.14 = (bf16[3,8,1152]{2,1,0:T(8,128)(2,1)S(1)}, bf16[3,8,1152]{2,1,0:T(8,128)(2,1)S(1)}, u32[]{:S(2)}, u32[]{:S(2)}) collective-permute-start(bf16[3,8,1152]{2,1,0:T(8,128)(2,1)S(1)} %get-tuple-element.89), channel_id=1, source_target_pairs={{0,4},{1,5},{2,6},{3,7},{4,0},{5,1},{6,2},{7,3},{8,12},{9,13},{10,... | collective-permute-start | bytes 165896 | tf_op jit(solution)/shard_map/ppermute | solution.py:274
  51.3 12.9 %collective-permute-start.15 = (bf16[3,8,1152]{2,1,0:T(8,128)(2,1)S(1)}, bf16[3,8,1152]{2,1,0:T(8,128)(2,1)S(1)}, u32[]{:S(2)}, u32[]{:S(2)}) collective-permute-start(bf16[3,8,1152]{2,1,0:T(8,128)(2,1)S(1)} %get-tuple-element.90), channel_id=1, source_target_pairs={{0,5},{1,4},{2,7},{3,6},{4,1},{5,0},{6,3},{7,2},{8,13},{9,12},{10,... | collective-permute-start | bytes 165896 | tf_op jit(solution)/shard_map/ppermute | solution.py:274
  55.8 9.1 %collective-permute-start.16 = (bf16[3,8,1152]{2,1,0:T(8,128)(2,1)S(1)}, bf16[3,8,1152]{2,1,0:T(8,128)(2,1)S(1)}, u32[]{:S(2)}, u32[]{:S(2)}) collective-permute-start(bf16[3,8,1152]{2,1,0:T(8,128)(2,1)S(1)} %get-tuple-element.91), channel_id=1, source_target_pairs={{0,6},{1,7},{2,4},{3,5},{4,2},{5,3},{6,0},{7,1},{8,14},{9,15},{10,... | collective-permute-start | bytes 165896 | tf_op jit(solution)/shard_map/ppermute | solution.py:274
  59.6 7.1 %collective-permute-start.17 = (bf16[3,8,1152]{2,1,0:T(8,128)(2,1)S(1)}, bf16[3,8,1152]{2,1,0:T(8,128)(2,1)S(1)}, u32[]{:S(2)}, u32[]{:S(2)}) collective-permute-start(bf16[3,8,1152]{2,1,0:T(8,128)(2,1)S(1)} %get-tuple-element.92), channel_id=1, source_target_pairs={{0,7},{1,6},{2,5},{3,4},{4,3},{5,2},{6,1},{7,0},{8,15},{9,14},{10,... | collective-permute-start | bytes 165896 | tf_op jit(solution)/shard_map/ppermute | solution.py:274
  59.7 7.0 %collective-permute-start.11 = (bf16[3,16,1152]{2,1,0:T(8,128)(2,1)S(1)}, bf16[3,16,1152]{2,1,0:T(8,128)(2,1)S(1)}, u32[]{:S(2)}, u32[]{:S(2)}) collective-permute-start(bf16[3,16,1152]{2,1,0:T(8,128)(2,1)S(1)} %get-tuple-element.86), channel_id=1, source_target_pairs={{0,1},{1,0},{2,3},{3,2},{4,5},{5,4},{6,7},{7,6},{8,9},{9,8},{10,11... | collective-permute-start | bytes 331784 | tf_op jit(solution)/shard_map/ppermute | solution.py:274
  62.2 5.7 %collective-permute-start.12 = (bf16[3,16,1152]{2,1,0:T(8,128)(2,1)S(1)}, bf16[3,16,1152]{2,1,0:T(8,128)(2,1)S(1)}, u32[]{:S(2)}, u32[]{:S(2)}) collective-permute-start(bf16[3,16,1152]{2,1,0:T(8,128)(2,1)S(1)} %get-tuple-element.87), channel_id=1, source_target_pairs={{0,2},{1,3},{2,0},{3,1},{4,6},{5,7},{6,4},{7,5},{8,10},{9,11},{10,... | collective-permute-start | bytes 331784 | tf_op jit(solution)/shard_map/ppermute | solution.py:274
  64.1 7.6 %collective-permute-start.13 = (bf16[3,16,1152]{2,1,0:T(8,128)(2,1)S(1)}, bf16[3,16,1152]{2,1,0:T(8,128)(2,1)S(1)}, u32[]{:S(2)}, u32[]{:S(2)}) collective-permute-start(bf16[3,16,1152]{2,1,0:T(8,128)(2,1)S(1)} %get-tuple-element.88), channel_id=1, source_target_pairs={{0,3},{1,2},{2,1},{3,0},{4,7},{5,6},{6,5},{7,4},{8,11},{9,10},{10,... | collective-permute-start | bytes 331784 | tf_op jit(solution)/shard_map/ppermute | solution.py:274
  65.0 6.7 %collective-permute-start.24 = (bf16[1,360,128]{2,1,0:T(8,128)(2,1)S(1)}, bf16[1,360,128]{2,1,0:T(8,128)(2,1)S(1)}, u32[]{:S(2)}, u32[]{:S(2)}) collective-permute-start(bf16[1,360,128]{2,1,0:T(8,128)(2,1)S(1)} %fusion.3), channel_id=1, source_target_pairs={{0,4},{1,5},{2,6},{3,7},{4,0},{5,1},{6,2},{7,3},{8,12},{9,13},{10,... | collective-permute-start | bytes 276488 | tf_op jit(solution)/shard_map/ppermute | solution.py:274

commit v3 on v2

--- a/solution.py
+++ b/solution.py
@@ -18,7 +18,6 @@
 
 VMEM = pl.BlockSpec(memory_space=pltpu.VMEM)
 HBM = pl.BlockSpec(memory_space=pltpu.HBM)
-SMEM = pl.BlockSpec(memory_space=pltpu.SMEM)
 
 
 def dot(a, b, along_a, along_b):
@@ -119,7 +118,7 @@
     rows, width = q_ref.shape
     text = k_ref.shape[0]
     heads = Heads(width)
-    keep = lax.broadcasted_iota(jnp.int32, (text, rows), 0) < len_ref[0]
+    keep = lax.broadcasted_iota(jnp.int32, (text, rows), 0) < len_ref[...]
     q, c, k, v = q_ref[...], c_ref[...], k_ref[...], v_ref[...]
     per = HEADS // groups
     rest = 2 * per * heads.size % LANES
@@ -237,7 +236,7 @@
         outs[3][i * span : (i + 1) * span, whole * LANES :] = last
 
 
-PARAMS = pltpu.CompilerParams(vmem_limit_bytes=16 << 20)
+PARAMS = pltpu.CompilerParams(vmem_limit_bytes=8 << 20)
 
 
 def cost(flops, moved):
@@ -250,6 +249,10 @@
 
 def f32(*shape):
     return jax.ShapeDtypeStruct(shape, jnp.float32)
+
+
+def halved(n):
+    return range(n // 2, n)
 
 
 def local(n, tq, tk, tv, tc, cq, cc, text_k, text_v, text_len):
@@ -277,14 +280,14 @@
         return pl.pallas_call(
             partial(cross_kernel, groups),
             out_shape=(bf16(rows, width),) + text_out,
-            in_specs=[SMEM] + [VMEM] * 4,
+            in_specs=[VMEM] * 5,
             out_specs=(VMEM,) * (1 + len(text_out)),
             cost_estimate=big,
             compiler_params=PARAMS,
             name="cross",
         )(*cross_args)
 
-    cross_args = (text_len, cq.reshape(rows, width), cc.reshape(rows, width), text_k, text_v)
+    cross_args = (text_len.reshape(1, 1), cq.reshape(rows, width), cc.reshape(rows, width), text_k, text_v)
 
     def temporal(messages, chunk, part, period, before, heights):
         count = len(messages)
@@ -314,7 +317,8 @@
     each = positions // n
     chunks = CHUNKS if each % (8 * CHUNKS) == 0 else 1
     part = each // chunks
-    near, far = range(n // 2), range(n // 2, n)
+    near = [k for k in range(n) if k not in halved(n)]
+    far = list(halved(n))
     plan = [(k, 0, each) for k in near] + [(k, c * part, part) for c in range(chunks) for k in far]
     messages = pl.pallas_call(
         partial(pack_kernel, each, plan),

time: 72.9 us -> 72.9 us (level)
  no operation moved by 1% of the time
where the time goes in v3:
time: 72.9 us; the launch traced here: 72.7 us
  starting transfers between devices  48.8 us (67%)
  waiting for transfers between devices  13.9 us (19%)
  Pallas kernels  7.47 us (10%)
  between operations  1.46 us (2%)
  local copies, waits for them, and re-layouts  1.02 us (1%)
    ppermute x25, starting transfers between devices, swap(): return lax.ppermute(x, AXIS, [(i, i ^ k) for i in range(n)])  48.8 us
    ppermute x25, waiting for transfers between devices, swap(): return lax.ppermute(x, AXIS, [(i, i ^ k) for i in range(n)])  13.9 us
    pallas_call x1, Pallas kernels, cross(): pl.pallas_call(partial(cross_kernel, groups), out_shape=(bf16(rows, width...  2.82 us
    pallas_call x2, Pallas kernels, temporal(): pl.pallas_call(partial(temporal_kernel, count, chunk, part, period), out_...  1.91 us
    pallas_call x1, Pallas kernels, local(): pl.pallas_call(partial(pack_kernel, each, plan), out_shape=tuple((bf16(4,...  1.71 us
  transfers between devices with their start and end apart: 25, of which 11 were waited for; matrix products, arithmetic and copies ran while one was open for 0% of the time, Pallas kernels for 3%

profile of v3, /device:TPU:0, one launch (start us, length us, event | category | flops | bytes accessed | tf_op | source)
XLA Modules:
  0.0 72.7 jit_solution(14902957085726614490)
XLA Ops:
  1.3 1.7 %pack.1 = (bf16[4,16,1152]{2,1,0:T(8,128)(2,1)S(1)}, bf16[4,16,1152]{2,1,0:T(8,128)(2,1)S(1)}, bf16[4,16,1152]{2,1,0:T(8,128)(2,1)S(1)}, bf16[4,16,1152]{2,1,0:T...) custom-call(bf16[128,1152]{1,0:T(8,128)(2,1)} %bitcast.31, ...), custom_call_target="tpu_custom_call" | custom-call | bytes 2359296 | tf_op jit(solution)/shard_map/pack/pallas_call | solution.py:323
  3.1 0.0 copy-start.3
  3.1 1.0 %copy-done.3 = bf16[1,128,1152]{2,1,0:T(8,128)(2,1)S(1)} copy-done((bf16[1,128,1152]{2,1,0:T(8,128)(2,1)S(1)}, bf16[1,128,1152]{2,1,0:T(8,128)(2,1)}, u32[]{:S(2)}) %copy-start.3) | copy-done | bytes 294936
  4.0 2.8 %cross.1 = (bf16[128,1152]{1,0:T(8,128)(2,1)}, f32[4,360,128]{2,1,0:T(8,128)S(1)}, bf16[4,360,128]{2,1,0:T(8,128)(2,1)S(1)}) custom-call(s32[1,1]{1,0:T(1,128)} %bitcast.26.len_ref, bf16[128,1152]{1,0:T(8,128)(2,1)S(1)} %bitcast.27, bf16[128,1152]{1,0:T(8,128)(2,1)S(1)} %bitcast.28, bf16[160,1152]{1,0:T(8,128)(2,1)S(1)} %copy-done, ...), custom_call_target="tpu_custom_call" | custom-call | flops 943718400 | bytes 1769472 | tf_op jit(solution)/shard_map/cross/pallas_call | solution.py:280
  6.9 3.0 %collective-permute-start.22 = (bf16[4,360,128]{2,1,0:T(8,128)(2,1)S(1)}, bf16[4,360,128]{2,1,0:T(8,128)(2,1)S(1)}, u32[]{:S(2)}, u32[]{:S(2)}) collective-permute-start(bf16[4,360,128]{2,1,0:T(8,128)(2,1)S(1)} %get-tuple-element.103), channel_id=1, source_target_pairs={{0,1},{1,0},{2,3},{3,2},{4,5},{5,4},{6,7},{7,6},{8,9},{9,8},{10,11... | collective-permute-start | bytes 1105928 | tf_op jit(solution)/shard_map/ppermute | solution.py:277
  9.8 2.6 %collective-permute-start.7 = (bf16[4,8,1152]{2,1,0:T(8,128)(2,1)S(1)}, bf16[4,8,1152]{2,1,0:T(8,128)(2,1)S(1)}, u32[]{:S(2)}, u32[]{:S(2)}) collective-permute-start(bf16[4,8,1152]{2,1,0:T(8,128)(2,1)S(1)} %get-tuple-element.77), channel_id=1, source_target_pairs={{0,4},{1,5},{2,6},{3,7},{4,0},{5,1},{6,2},{7,3},{8,12},{9,13},{10,... | collective-permute-start | bytes 221192 | tf_op jit(solution)/shard_map/ppermute | solution.py:277
  12.4 0.0 collective-permute-start.8
  12.4 3.9 %collective-permute-start.9 = (bf16[4,8,1152]{2,1,0:T(8,128)(2,1)S(1)}, bf16[4,8,1152]{2,1,0:T(8,128)(2,1)S(1)}, u32[]{:S(2)}, u32[]{:S(2)}) collective-permute-start(bf16[4,8,1152]{2,1,0:T(8,128)(2,1)S(1)} %get-tuple-element.79), channel_id=1, source_target_pairs={{0,6},{1,7},{2,4},{3,5},{4,2},{5,3},{6,0},{7,1},{8,14},{9,15},{10,... | collective-permute-start | bytes 221192 | tf_op jit(solution)/shard_map/ppermute | solution.py:277
  16.3 1.2 %collective-permute-start.10 = (bf16[4,8,1152]{2,1,0:T(8,128)(2,1)S(1)}, bf16[4,8,1152]{2,1,0:T(8,128)(2,1)S(1)}, u32[]{:S(2)}, u32[]{:S(2)}) collective-permute-start(bf16[4,8,1152]{2,1,0:T(8,128)(2,1)S(1)} %get-tuple-element.80), channel_id=1, source_target_pairs={{0,7},{1,6},{2,5},{3,4},{4,3},{5,2},{6,1},{7,0},{8,15},{9,14},{10,... | collective-permute-start | bytes 221192 | tf_op jit(solution)/shard_map/ppermute | solution.py:277
  17.5 1.7 %collective-permute-done.22 = bf16[4,360,128]{2,1,0:T(8,128)(2,1)S(1)} collective-permute-done((bf16[4,360,128]{2,1,0:T(8,128)(2,1)S(1)}, bf16[4,360,128]{2,1,0:T(8,128)(2,1)S(1)}, u32[]{:S(2)}, u32[]{:S(2)}) %collective-permute-start.22) | collective-permute-done | bytes 368672 | tf_op jit(solution)/shard_map/ppermute | solution.py:277
  19.2 1.1 %collective-permute-start = (bf16[4,16,1152]{2,1,0:T(8,128)(2,1)S(1)}, bf16[4,16,1152]{2,1,0:T(8,128)(2,1)S(1)}, u32[]{:S(2)}, u32[]{:S(2)}) collective-permute-start(bf16[4,16,1152]{2,1,0:T(8,128)(2,1)S(1)} %get-tuple-element.70), channel_id=1, source_target_pairs={{0,1},{1,0},{2,3},{3,2},{4,5},{5,4},{6,7},{7,6},{8,9},{9,8},{10,11... | collective-permute-start | bytes 442376 | tf_op jit(solution)/shard_map/ppermute | solution.py:277
  20.3 0.1 convert_add_fusion
  20.4 0.0 collective-permute-done.7.refs_4_
  20.4 3.1 %collective-permute-start.1 = (bf16[4,16,1152]{2,1,0:T(8,128)(2,1)S(1)}, bf16[4,16,1152]{2,1,0:T(8,128)(2,1)S(1)}, u32[]{:S(2)}, u32[]{:S(2)}) collective-permute-start(bf16[4,16,1152]{2,1,0:T(8,128)(2,1)S(1)} %get-tuple-element.71), channel_id=1, source_target_pairs={{0,2},{1,3},{2,0},{3,1},{4,6},{5,7},{6,4},{7,5},{8,10},{9,11},{10,... | collective-permute-start | bytes 442376 | tf_op jit(solution)/shard_map/ppermute | solution.py:277
  23.4 0.1 collective-permute-done.8.refs_5_
  23.5 0.0 collective-permute-start.2
  23.6 0.0 collective-permute-done.9.refs_6_
  23.6 2.0 %collective-permute-start.23 = (bf16[2,360,128]{2,1,0:T(8,128)(2,1)S(1)}, bf16[2,360,128]{2,1,0:T(8,128)(2,1)S(1)}, u32[]{:S(2)}, u32[]{:S(2)}) collective-permute-start(bf16[2,360,128]{2,1,0:T(8,128)(2,1)S(1)} %fusion.2), channel_id=1, source_target_pairs={{0,2},{1,3},{2,0},{3,1},{4,6},{5,7},{6,4},{7,5},{8,10},{9,11},{10,... | collective-permute-start | bytes 552968 | tf_op jit(solution)/shard_map/ppermute | solution.py:277
  25.6 2.6 %collective-permute-start.3 = (bf16[4,8,1152]{2,1,0:T(8,128)(2,1)S(1)}, bf16[4,8,1152]{2,1,0:T(8,128)(2,1)S(1)}, u32[]{:S(2)}, u32[]{:S(2)}) collective-permute-start(bf16[4,8,1152]{2,1,0:T(8,128)(2,1)S(1)} %get-tuple-element.73), channel_id=1, source_target_pairs={{0,4},{1,5},{2,6},{3,7},{4,0},{5,1},{6,2},{7,3},{8,12},{9,13},{10,... | collective-permute-start | bytes 221192 | tf_op jit(solution)/shard_map/ppermute | solution.py:277
  28.2 0.0 collective-permute-done.refs_1_
  28.2 3.9 %collective-permute-start.4 = (bf16[4,8,1152]{2,1,0:T(8,128)(2,1)S(1)}, bf16[4,8,1152]{2,1,0:T(8,128)(2,1)S(1)}, u32[]{:S(2)}, u32[]{:S(2)}) collective-permute-start(bf16[4,8,1152]{2,1,0:T(8,128)(2,1)S(1)} %get-tuple-element.74), channel_id=1, source_target_pairs={{0,5},{1,4},{2,7},{3,6},{4,1},{5,0},{6,3},{7,2},{8,13},{9,12},{10,... | collective-permute-start | bytes 221192 | tf_op jit(solution)/shard_map/ppermute | solution.py:277
  32.1 0.0 collective-permute-done.1.refs_2_
  32.1 0.9 %collective-permute-start.5 = (bf16[4,8,1152]{2,1,0:T(8,128)(2,1)S(1)}, bf16[4,8,1152]{2,1,0:T(8,128)(2,1)S(1)}, u32[]{:S(2)}, u32[]{:S(2)}) collective-permute-start(bf16[4,8,1152]{2,1,0:T(8,128)(2,1)S(1)} %get-tuple-element.75), channel_id=1, source_target_pairs={{0,6},{1,7},{2,4},{3,5},{4,2},{5,3},{6,0},{7,1},{8,14},{9,15},{10,... | collective-permute-start | bytes 221192 | tf_op jit(solution)/shard_map/ppermute | solution.py:277
  33.0 0.5 collective-permute-done.2.refs_3_
  33.5 6.1 %collective-permute-start.6 = (bf16[4,8,1152]{2,1,0:T(8,128)(2,1)S(1)}, bf16[4,8,1152]{2,1,0:T(8,128)(2,1)S(1)}, u32[]{:S(2)}, u32[]{:S(2)}) collective-permute-start(bf16[4,8,1152]{2,1,0:T(8,128)(2,1)S(1)} %get-tuple-element.76), channel_id=1, source_target_pairs={{0,7},{1,6},{2,5},{3,4},{4,3},{5,2},{6,1},{7,0},{8,15},{9,14},{10,... | collective-permute-start | bytes 221192 | tf_op jit(solution)/shard_map/ppermute | solution.py:277
  39.6 0.9 %shard_map.128 = (bf16[3,8,1152]{2,1,0:T(8,128)(2,1)S(1)}, bf16[3,8,1152]{2,1,0:T(8,128)(2,1)S(1)}, bf16[3,8,1152]{2,1,0:T(8,128)(2,1)S(1)}, bf16[3,8,1152]{2,1,...) custom-call(bf16[4,16,1152]{2,1,0:T(8,128)(2,1)S(1)} %get-tuple-elem, ...), custom_call_target="tpu_custom_call" | custom-call | flops 943718400 | bytes 1769472 | tf_op jit(solution)/shard_map/pallas_call | solution.py:294
  40.5 0.0 collective-permute-done.3.refs_4_
  40.6 0.5 collective-permute-done.5.refs_6_
  41.1 1.4 %collective-permute-done.6.refs_7_ = bf16[4,8,1152]{2,1,0:T(8,128)(2,1)S(1)} collective-permute-done((bf16[4,8,1152]{2,1,0:T(8,128)(2,1)S(1)}, bf16[4,8,1152]{2,1,0:T(8,128)(2,1)S(1)}, u32[]{:S(2)}, u32[]{:S(2)}) %collective-permute-start.6) | collective-permute-done | bytes 73760 | tf_op jit(solution)/shard_map/ppermute | solution.py:277
  42.5 1.0 %shard_map.129 = (bf16[3,16,1152]{2,1,0:T(8,128)(2,1)S(1)}, bf16[3,16,1152]{2,1,0:T(8,128)(2,1)S(1)}, bf16[3,16,1152]{2,1,0:T(8,128)(2,1)S(1)}, bf16[3,16,1152]{...) custom-call(bf16[4,16,1152]{2,1,0:T(8,128)(2,1)S(1)} %get-tuple-elem, ...), custom_call_target="tpu_custom_call" | custom-call | flops 943718400 | bytes 1769472 | tf_op jit(solution)/shard_map/pallas_call | solution.py:294
  43.5 1.4 %collective-permute-start.18 = (bf16[3,8,1152]{2,1,0:T(8,128)(2,1)S(1)}, bf16[3,8,1152]{2,1,0:T(8,128)(2,1)S(1)}, u32[]{:S(2)}, u32[]{:S(2)}) collective-permute-start(bf16[3,8,1152]{2,1,0:T(8,128)(2,1)S(1)} %get-tuple-element.93), channel_id=1, source_target_pairs={{0,4},{1,5},{2,6},{3,7},{4,0},{5,1},{6,2},{7,3},{8,12},{9,13},{10,... | collective-permute-start | bytes 165896 | tf_op jit(solution)/shard_map/ppermute | solution.py:277
  44.9 1.8 %collective-permute-start.19 = (bf16[3,8,1152]{2,1,0:T(8,128)(2,1)S(1)}, bf16[3,8,1152]{2,1,0:T(8,128)(2,1)S(1)}, u32[]{:S(2)}, u32[]{:S(2)}) collective-permute-start(bf16[3,8,1152]{2,1,0:T(8,128)(2,1)S(1)} %get-tuple-element.94), channel_id=1, source_target_pairs={{0,5},{1,4},{2,7},{3,6},{4,1},{5,0},{6,3},{7,2},{8,13},{9,12},{10,... | collective-permute-start | bytes 165896 | tf_op jit(solution)/shard_map/ppermute | solution.py:277
  46.7 3.9 %collective-permute-start.20 = (bf16[3,8,1152]{2,1,0:T(8,128)(2,1)S(1)}, bf16[3,8,1152]{2,1,0:T(8,128)(2,1)S(1)}, u32[]{:S(2)}, u32[]{:S(2)}) collective-permute-start(bf16[3,8,1152]{2,1,0:T(8,128)(2,1)S(1)} %get-tuple-element.95), channel_id=1, source_target_pairs={{0,6},{1,7},{2,4},{3,5},{4,2},{5,3},{6,0},{7,1},{8,14},{9,15},{10,... | collective-permute-start | bytes 165896 | tf_op jit(solution)/shard_map/ppermute | solution.py:277
  50.6 0.6 collective-permute-start.21
  51.3 3.3 %collective-permute-start.15 = (bf16[3,8,1152]{2,1,0:T(8,128)(2,1)S(1)}, bf16[3,8,1152]{2,1,0:T(8,128)(2,1)S(1)}, u32[]{:S(2)}, u32[]{:S(2)}) collective-permute-start(bf16[3,8,1152]{2,1,0:T(8,128)(2,1)S(1)} %get-tuple-element.90), channel_id=1, source_target_pairs={{0,5},{1,4},{2,7},{3,6},{4,1},{5,0},{6,3},{7,2},{8,13},{9,12},{10,... | collective-permute-start | bytes 165896 | tf_op jit(solution)/shard_map/ppermute | solution.py:277
  54.5 1.3 %collective-permute-done.19.refs_9_ = bf16[3,8,1152]{2,1,0:T(8,128)(2,1)S(1)} collective-permute-done((bf16[3,8,1152]{2,1,0:T(8,128)(2,1)S(1)}, bf16[3,8,1152]{2,1,0:T(8,128)(2,1)S(1)}, u32[]{:S(2)}, u32[]{:S(2)}) %collective-permute-start.19) | collective-permute-done | bytes 55328 | tf_op jit(solution)/shard_map/ppermute | solution.py:277
  55.8 3.7 %collective-permute-start.16 = (bf16[3,8,1152]{2,1,0:T(8,128)(2,1)S(1)}, bf16[3,8,1152]{2,1,0:T(8,128)(2,1)S(1)}, u32[]{:S(2)}, u32[]{:S(2)}) collective-permute-start(bf16[3,8,1152]{2,1,0:T(8,128)(2,1)S(1)} %get-tuple-element.91), channel_id=1, source_target_pairs={{0,6},{1,7},{2,4},{3,5},{4,2},{5,3},{6,0},{7,1},{8,14},{9,15},{10,... | collective-permute-start | bytes 165896 | tf_op jit(solution)/shard_map/ppermute | solution.py:277
  59.6 0.1 collective-permute-start.17
  59.7 1.5 %collective-permute-start.11 = (bf16[3,16,1152]{2,1,0:T(8,128)(2,1)S(1)}, bf16[3,16,1152]{2,1,0:T(8,128)(2,1)S(1)}, u32[]{:S(2)}, u32[]{:S(2)}) collective-permute-start(bf16[3,16,1152]{2,1,0:T(8,128)(2,1)S(1)} %get-tuple-element.86), channel_id=1, source_target_pairs={{0,1},{1,0},{2,3},{3,2},{4,5},{5,4},{6,7},{7,6},{8,9},{9,8},{10,11... | collective-permute-start | bytes 331784 | tf_op jit(solution)/shard_map/ppermute | solution.py:277
  61.2 1.1 %collective-permute-done.14.refs_4_ = bf16[3,8,1152]{2,1,0:T(8,128)(2,1)S(1)} collective-permute-done((bf16[3,8,1152]{2,1,0:T(8,128)(2,1)S(1)}, bf16[3,8,1152]{2,1,0:T(8,128)(2,1)S(1)}, u32[]{:S(2)}, u32[]{:S(2)}) %collective-permute-start.14) | collective-permute-done | bytes 55328 | tf_op jit(solution)/shard_map/ppermute | solution.py:277
  62.2 0.1 collective-permute-start.12
  62.3 1.8 %collective-permute-done.15.refs_5_ = bf16[3,8,1152]{2,1,0:T(8,128)(2,1)S(1)} collective-permute-done((bf16[3,8,1152]{2,1,0:T(8,128)(2,1)S(1)}, bf16[3,8,1152]{2,1,0:T(8,128)(2,1)S(1)}, u32[]{:S(2)}, u32[]{:S(2)}) %collective-permute-start.15) | collective-permute-done | bytes 55328 | tf_op jit(solution)/shard_map/ppermute | solution.py:277
  64.1 0.8 %collective-permute-start.13 = (bf16[3,16,1152]{2,1,0:T(8,128)(2,1)S(1)}, bf16[3,16,1152]{2,1,0:T(8,128)(2,1)S(1)}, u32[]{:S(2)}, u32[]{:S(2)}) collective-permute-start(bf16[3,16,1152]{2,1,0:T(8,128)(2,1)S(1)} %get-tuple-element.88), channel_id=1, source_target_pairs={{0,3},{1,2},{2,1},{3,0},{4,7},{5,6},{6,5},{7,4},{8,11},{9,10},{10,... | collective-permute-start | bytes 331784 | tf_op jit(solution)/shard_map/ppermute | solution.py:277
  65.0 1.3 %collective-permute-start.24 = (bf16[1,360,128]{2,1,0:T(8,128)(2,1)S(1)}, bf16[1,360,128]{2,1,0:T(8,128)(2,1)S(1)}, u32[]{:S(2)}, u32[]{:S(2)}) collective-permute-start(bf16[1,360,128]{2,1,0:T(8,128)(2,1)S(1)} %fusion.3), channel_id=1, source_target_pairs={{0,4},{1,5},{2,6},{3,7},{4,0},{5,1},{6,2},{7,3},{8,12},{9,13},{10,... | collective-permute-start | bytes 276488 | tf_op jit(solution)/shard_map/ppermute | solution.py:277
  66.3 0.4 collective-permute-done.17.refs_7_
  66.7 1.3 %collective-permute-done.12.refs_2_ = bf16[3,16,1152]{2,1,0:T(8,128)(2,1)S(1)} collective-permute-done((bf16[3,16,1152]{2,1,0:T(8,128)(2,1)S(1)}, bf16[3,16,1152]{2,1,0:T(8,128)(2,1)S(1)}, u32[]{:S(2)}, u32[]{:S(2)}) %collective-permute-start.12) | collective-permute-done | bytes 110624 | tf_op jit(solution)/shard_map/ppermute | solution.py:277
  67.9 3.8 %collective-permute-done.13.refs_3_ = bf16[3,16,1152]{2,1,0:T(8,128)(2,1)S(1)} collective-permute-done((bf16[3,16,1152]{2,1,0:T(8,128)(2,1)S(1)}, bf16[3,16,1152]{2,1,0:T(8,128)(2,1)S(1)}, u32[]{:S(2)}, u32[]{:S(2)}) %collective-permute-start.13) | collective-permute-done | bytes 110624 | tf_op jit(solution)/shard_map/ppermute | solution.py:277
  71.7 1.0 %unpack.1 = (bf16[128,1152]{1,0:T(8,128)(2,1)}, bf16[128,1152]{1,0:T(8,128)(2,1)}, bf16[128,1152]{1,0:T(8,128)(2,1)}, f32[160,288]{1,0:T(8,128)}) custom-call(bf16[3,16,1152]{2,1,0:T(8,128)(2,1)S(1)} %get-tuple-element.85.refs_0_, bf16[3,16,1152]{2,1,0:T(8,128)(2,1)S(1)} %collective-permute-done.11.refs_1_, ...), custom_call_target="tpu_custom_call" | custom-call | bytes 1769472 | tf_op jit(solution)/shard_map/unpack/pallas_call | solution.py:365
  (20 shorter events, 0.1 us)
Async XLA Ops:
  1.3 1.8 %copy-start = (bf16[160,1152]{1,0:T(8,128)(2,1)S(1)}, bf16[160,1152]{1,0:T(8,128)(2,1)}, u32[]{:S(2)}) copy-start(bf16[160,1152]{1,0:T(8,128)(2,1)} %k_ref) | copy-start | bytes 1105924
  1.3 1.8 %copy-start.1 = (bf16[160,1152]{1,0:T(8,128)(2,1)S(1)}, bf16[160,1152]{1,0:T(8,128)(2,1)}, u32[]{:S(2)}) copy-start(bf16[160,1152]{1,0:T(8,128)(2,1)} %v_ref) | copy-start | bytes 1105924
  1.3 1.8 %copy-start.2 = (bf16[1,128,1152]{2,1,0:T(8,128)(2,1)S(1)}, bf16[1,128,1152]{2,1,0:T(8,128)(2,1)}, u32[]{:S(2)}) copy-start(bf16[1,128,1152]{2,1,0:T(8,128)(2,1)} %param.13) | copy-start | bytes 884740
  3.1 1.0 %copy-start.3 = (bf16[1,128,1152]{2,1,0:T(8,128)(2,1)S(1)}, bf16[1,128,1152]{2,1,0:T(8,128)(2,1)}, u32[]{:S(2)}) copy-start(bf16[1,128,1152]{2,1,0:T(8,128)(2,1)} %param.14) | copy-start | bytes 884740
  6.9 12.4 %collective-permute-start.22 = (bf16[4,360,128]{2,1,0:T(8,128)(2,1)S(1)}, bf16[4,360,128]{2,1,0:T(8,128)(2,1)S(1)}, u32[]{:S(2)}, u32[]{:S(2)}) collective-permute-start(bf16[4,360,128]{2,1,0:T(8,128)(2,1)S(1)} %get-tuple-element.103), channel_id=1, source_target_pairs={{0,1},{1,0},{2,3},{3,2},{4,5},{5,4},{6,7},{7,6},{8,9},{9,8},{10,11... | collective-permute-start | bytes 1105928 | tf_op jit(solution)/shard_map/ppermute | solution.py:277
  9.8 10.6 %collective-permute-start.7 = (bf16[4,8,1152]{2,1,0:T(8,128)(2,1)S(1)}, bf16[4,8,1152]{2,1,0:T(8,128)(2,1)S(1)}, u32[]{:S(2)}, u32[]{:S(2)}) collective-permute-start(bf16[4,8,1152]{2,1,0:T(8,128)(2,1)S(1)} %get-tuple-element.77), channel_id=1, source_target_pairs={{0,4},{1,5},{2,6},{3,7},{4,0},{5,1},{6,2},{7,3},{8,12},{9,13},{10,... | collective-permute-start | bytes 221192 | tf_op jit(solution)/shard_map/ppermute | solution.py:277
  12.4 11.1 %collective-permute-start.8 = (bf16[4,8,1152]{2,1,0:T(8,128)(2,1)S(1)}, bf16[4,8,1152]{2,1,0:T(8,128)(2,1)S(1)}, u32[]{:S(2)}, u32[]{:S(2)}) collective-permute-start(bf16[4,8,1152]{2,1,0:T(8,128)(2,1)S(1)} %get-tuple-element.78), channel_id=1, source_target_pairs={{0,5},{1,4},{2,7},{3,6},{4,1},{5,0},{6,3},{7,2},{8,13},{9,12},{10,... | collective-permute-start | bytes 221192 | tf_op jit(solution)/shard_map/ppermute | solution.py:277
  12.4 11.2 %collective-permute-start.9 = (bf16[4,8,1152]{2,1,0:T(8,128)(2,1)S(1)}, bf16[4,8,1152]{2,1,0:T(8,128)(2,1)S(1)}, u32[]{:S(2)}, u32[]{:S(2)}) collective-permute-start(bf16[4,8,1152]{2,1,0:T(8,128)(2,1)S(1)} %get-tuple-element.79), channel_id=1, source_target_pairs={{0,6},{1,7},{2,4},{3,5},{4,2},{5,3},{6,0},{7,1},{8,14},{9,15},{10,... | collective-permute-start | bytes 221192 | tf_op jit(solution)/shard_map/ppermute | solution.py:277
  16.3 9.2 %collective-permute-start.10 = (bf16[4,8,1152]{2,1,0:T(8,128)(2,1)S(1)}, bf16[4,8,1152]{2,1,0:T(8,128)(2,1)S(1)}, u32[]{:S(2)}, u32[]{:S(2)}) collective-permute-start(bf16[4,8,1152]{2,1,0:T(8,128)(2,1)S(1)} %get-tuple-element.80), channel_id=1, source_target_pairs={{0,7},{1,6},{2,5},{3,4},{4,3},{5,2},{6,1},{7,0},{8,15},{9,14},{10,... | collective-permute-start | bytes 221192 | tf_op jit(solution)/shard_map/ppermute | solution.py:277
  19.2 9.0 %collective-permute-start = (bf16[4,16,1152]{2,1,0:T(8,128)(2,1)S(1)}, bf16[4,16,1152]{2,1,0:T(8,128)(2,1)S(1)}, u32[]{:S(2)}, u32[]{:S(2)}) collective-permute-start(bf16[4,16,1152]{2,1,0:T(8,128)(2,1)S(1)} %get-tuple-element.70), channel_id=1, source_target_pairs={{0,1},{1,0},{2,3},{3,2},{4,5},{5,4},{6,7},{7,6},{8,9},{9,8},{10,11... | collective-permute-start | bytes 442376 | tf_op jit(solution)/shard_map/ppermute | solution.py:277
  20.4 11.7 %collective-permute-start.1 = (bf16[4,16,1152]{2,1,0:T(8,128)(2,1)S(1)}, bf16[4,16,1152]{2,1,0:T(8,128)(2,1)S(1)}, u32[]{:S(2)}, u32[]{:S(2)}) collective-permute-start(bf16[4,16,1152]{2,1,0:T(8,128)(2,1)S(1)} %get-tuple-element.71), channel_id=1, source_target_pairs={{0,2},{1,3},{2,0},{3,1},{4,6},{5,7},{6,4},{7,5},{8,10},{9,11},{10,... | collective-permute-start | bytes 442376 | tf_op jit(solution)/shard_map/ppermute | solution.py:277
  23.5 10.0 %collective-permute-start.2 = (bf16[4,16,1152]{2,1,0:T(8,128)(2,1)S(1)}, bf16[4,16,1152]{2,1,0:T(8,128)(2,1)S(1)}, u32[]{:S(2)}, u32[]{:S(2)}) collective-permute-start(bf16[4,16,1152]{2,1,0:T(8,128)(2,1)S(1)} %get-tuple-element.72), channel_id=1, source_target_pairs={{0,3},{1,2},{2,1},{3,0},{4,7},{5,6},{6,5},{7,4},{8,11},{9,10},{10,... | collective-permute-start | bytes 442376 | tf_op jit(solution)/shard_map/ppermute | solution.py:277
  23.6 27.6 %collective-permute-start.23 = (bf16[2,360,128]{2,1,0:T(8,128)(2,1)S(1)}, bf16[2,360,128]{2,1,0:T(8,128)(2,1)S(1)}, u32[]{:S(2)}, u32[]{:S(2)}) collective-permute-start(bf16[2,360,128]{2,1,0:T(8,128)(2,1)S(1)} %fusion.2), channel_id=1, source_target_pairs={{0,2},{1,3},{2,0},{3,1},{4,6},{5,7},{6,4},{7,5},{8,10},{9,11},{10,... | collective-permute-start | bytes 552968 | tf_op jit(solution)/shard_map/ppermute | solution.py:277
  25.6 15.0 %collective-permute-start.3 = (bf16[4,8,1152]{2,1,0:T(8,128)(2,1)S(1)}, bf16[4,8,1152]{2,1,0:T(8,128)(2,1)S(1)}, u32[]{:S(2)}, u32[]{:S(2)}) collective-permute-start(bf16[4,8,1152]{2,1,0:T(8,128)(2,1)S(1)} %get-tuple-element.73), channel_id=1, source_target_pairs={{0,4},{1,5},{2,6},{3,7},{4,0},{5,1},{6,2},{7,3},{8,12},{9,13},{10,... | collective-permute-start | bytes 221192 | tf_op jit(solution)/shard_map/ppermute | solution.py:277
  28.2 12.4 %collective-permute-start.4 = (bf16[4,8,1152]{2,1,0:T(8,128)(2,1)S(1)}, bf16[4,8,1152]{2,1,0:T(8,128)(2,1)S(1)}, u32[]{:S(2)}, u32[]{:S(2)}) collective-permute-start(bf16[4,8,1152]{2,1,0:T(8,128)(2,1)S(1)} %get-tuple-element.74), channel_id=1, source_target_pairs={{0,5},{1,4},{2,7},{3,6},{4,1},{5,0},{6,3},{7,2},{8,13},{9,12},{10,... | collective-permute-start | bytes 221192 | tf_op jit(solution)/shard_map/ppermute | solution.py:277
  32.1 9.0 %collective-permute-start.5 = (bf16[4,8,1152]{2,1,0:T(8,128)(2,1)S(1)}, bf16[4,8,1152]{2,1,0:T(8,128)(2,1)S(1)}, u32[]{:S(2)}, u32[]{:S(2)}) collective-permute-start(bf16[4,8,1152]{2,1,0:T(8,128)(2,1)S(1)} %get-tuple-element.75), channel_id=1, source_target_pairs={{0,6},{1,7},{2,4},{3,5},{4,2},{5,3},{6,0},{7,1},{8,14},{9,15},{10,... | collective-permute-start | bytes 221192 | tf_op jit(solution)/shard_map/ppermute | solution.py:277
  33.5 9.0 %collective-permute-start.6 = (bf16[4,8,1152]{2,1,0:T(8,128)(2,1)S(1)}, bf16[4,8,1152]{2,1,0:T(8,128)(2,1)S(1)}, u32[]{:S(2)}, u32[]{:S(2)}) collective-permute-start(bf16[4,8,1152]{2,1,0:T(8,128)(2,1)S(1)} %get-tuple-element.76), channel_id=1, source_target_pairs={{0,7},{1,6},{2,5},{3,4},{4,3},{5,2},{6,1},{7,0},{8,15},{9,14},{10,... | collective-permute-start | bytes 221192 | tf_op jit(solution)/shard_map/ppermute | solution.py:277
  43.5 7.8 %collective-permute-start.18 = (bf16[3,8,1152]{2,1,0:T(8,128)(2,1)S(1)}, bf16[3,8,1152]{2,1,0:T(8,128)(2,1)S(1)}, u32[]{:S(2)}, u32[]{:S(2)}) collective-permute-start(bf16[3,8,1152]{2,1,0:T(8,128)(2,1)S(1)} %get-tuple-element.93), channel_id=1, source_target_pairs={{0,4},{1,5},{2,6},{3,7},{4,0},{5,1},{6,2},{7,3},{8,12},{9,13},{10,... | collective-permute-start | bytes 165896 | tf_op jit(solution)/shard_map/ppermute | solution.py:277
  44.9 10.9 %collective-permute-start.19 = (bf16[3,8,1152]{2,1,0:T(8,128)(2,1)S(1)}, bf16[3,8,1152]{2,1,0:T(8,128)(2,1)S(1)}, u32[]{:S(2)}, u32[]{:S(2)}) collective-permute-start(bf16[3,8,1152]{2,1,0:T(8,128)(2,1)S(1)} %get-tuple-element.94), channel_id=1, source_target_pairs={{0,5},{1,4},{2,7},{3,6},{4,1},{5,0},{6,3},{7,2},{8,13},{9,12},{10,... | collective-permute-start | bytes 165896 | tf_op jit(solution)/shard_map/ppermute | solution.py:277
  46.7 12.8 %collective-permute-start.20 = (bf16[3,8,1152]{2,1,0:T(8,128)(2,1)S(1)}, bf16[3,8,1152]{2,1,0:T(8,128)(2,1)S(1)}, u32[]{:S(2)}, u32[]{:S(2)}) collective-permute-start(bf16[3,8,1152]{2,1,0:T(8,128)(2,1)S(1)} %get-tuple-element.95), channel_id=1, source_target_pairs={{0,6},{1,7},{2,4},{3,5},{4,2},{5,3},{6,0},{7,1},{8,14},{9,15},{10,... | collective-permute-start | bytes 165896 | tf_op jit(solution)/shard_map/ppermute | solution.py:277
  50.6 9.1 %collective-permute-start.21 = (bf16[3,8,1152]{2,1,0:T(8,128)(2,1)S(1)}, bf16[3,8,1152]{2,1,0:T(8,128)(2,1)S(1)}, u32[]{:S(2)}, u32[]{:S(2)}) collective-permute-start(bf16[3,8,1152]{2,1,0:T(8,128)(2,1)S(1)} %get-tuple-element.96), channel_id=1, source_target_pairs={{0,7},{1,6},{2,5},{3,4},{4,3},{5,2},{6,1},{7,0},{8,15},{9,14},{10,... | collective-permute-start | bytes 165896 | tf_op jit(solution)/shard_map/ppermute | solution.py:277
  51.2 11.0 %collective-permute-start.14 = (bf16[3,8,1152]{2,1,0:T(8,128)(2,1)S(1)}, bf16[3,8,1152]{2,1,0:T(8,128)(2,1)S(1)}, u32[]{:S(2)}, u32[]{:S(2)}) collective-permute-start(bf16[3,8,1152]{2,1,0:T(8,128)(2,1)S(1)} %get-tuple-element.89), channel_id=1, source_target_pairs={{0,4},{1,5},{2,6},{3,7},{4,0},{5,1},{6,2},{7,3},{8,12},{9,13},{10,... | collective-permute-start | bytes 165896 | tf_op jit(solution)/shard_map/ppermute | solution.py:277
  51.3 12.8 %collective-permute-start.15 = (bf16[3,8,1152]{2,1,0:T(8,128)(2,1)S(1)}, bf16[3,8,1152]{2,1,0:T(8,128)(2,1)S(1)}, u32[]{:S(2)}, u32[]{:S(2)}) collective-permute-start(bf16[3,8,1152]{2,1,0:T(8,128)(2,1)S(1)} %get-tuple-element.90), channel_id=1, source_target_pairs={{0,5},{1,4},{2,7},{3,6},{4,1},{5,0},{6,3},{7,2},{8,13},{9,12},{10,... | collective-permute-start | bytes 165896 | tf_op jit(solution)/shard_map/ppermute | solution.py:277
  55.8 9.1 %collective-permute-start.16 = (bf16[3,8,1152]{2,1,0:T(8,128)(2,1)S(1)}, bf16[3,8,1152]{2,1,0:T(8,128)(2,1)S(1)}, u32[]{:S(2)}, u32[]{:S(2)}) collective-permute-start(bf16[3,8,1152]{2,1,0:T(8,128)(2,1)S(1)} %get-tuple-element.91), channel_id=1, source_target_pairs={{0,6},{1,7},{2,4},{3,5},{4,2},{5,3},{6,0},{7,1},{8,14},{9,15},{10,... | collective-permute-start | bytes 165896 | tf_op jit(solution)/shard_map/ppermute | solution.py:277
  59.6 7.1 %collective-permute-start.17 = (bf16[3,8,1152]{2,1,0:T(8,128)(2,1)S(1)}, bf16[3,8,1152]{2,1,0:T(8,128)(2,1)S(1)}, u32[]{:S(2)}, u32[]{:S(2)}) collective-permute-start(bf16[3,8,1152]{2,1,0:T(8,128)(2,1)S(1)} %get-tuple-element.92), channel_id=1, source_target_pairs={{0,7},{1,6},{2,5},{3,4},{4,3},{5,2},{6,1},{7,0},{8,15},{9,14},{10,... | collective-permute-start | bytes 165896 | tf_op jit(solution)/shard_map/ppermute | solution.py:277
  59.7 7.0 %collective-permute-start.11 = (bf16[3,16,1152]{2,1,0:T(8,128)(2,1)S(1)}, bf16[3,16,1152]{2,1,0:T(8,128)(2,1)S(1)}, u32[]{:S(2)}, u32[]{:S(2)}) collective-permute-start(bf16[3,16,1152]{2,1,0:T(8,128)(2,1)S(1)} %get-tuple-element.86), channel_id=1, source_target_pairs={{0,1},{1,0},{2,3},{3,2},{4,5},{5,4},{6,7},{7,6},{8,9},{9,8},{10,11... | collective-permute-start | bytes 331784 | tf_op jit(solution)/shard_map/ppermute | solution.py:277
  62.2 5.7 %collective-permute-start.12 = (bf16[3,16,1152]{2,1,0:T(8,128)(2,1)S(1)}, bf16[3,16,1152]{2,1,0:T(8,128)(2,1)S(1)}, u32[]{:S(2)}, u32[]{:S(2)}) collective-permute-start(bf16[3,16,1152]{2,1,0:T(8,128)(2,1)S(1)} %get-tuple-element.87), channel_id=1, source_target_pairs={{0,2},{1,3},{2,0},{3,1},{4,6},{5,7},{6,4},{7,5},{8,10},{9,11},{10,... | collective-permute-start | bytes 331784 | tf_op jit(solution)/shard_map/ppermute | solution.py:277
  64.1 7.6 %collective-permute-start.13 = (bf16[3,16,1152]{2,1,0:T(8,128)(2,1)S(1)}, bf16[3,16,1152]{2,1,0:T(8,128)(2,1)S(1)}, u32[]{:S(2)}, u32[]{:S(2)}) collective-permute-start(bf16[3,16,1152]{2,1,0:T(8,128)(2,1)S(1)} %get-tuple-element.88), channel_id=1, source_target_pairs={{0,3},{1,2},{2,1},{3,0},{4,7},{5,6},{6,5},{7,4},{8,11},{9,10},{10,... | collective-permute-start | bytes 331784 | tf_op jit(solution)/shard_map/ppermute | solution.py:277
  65.0 6.8 %collective-permute-start.24 = (bf16[1,360,128]{2,1,0:T(8,128)(2,1)S(1)}, bf16[1,360,128]{2,1,0:T(8,128)(2,1)S(1)}, u32[]{:S(2)}, u32[]{:S(2)}) collective-permute-start(bf16[1,360,128]{2,1,0:T(8,128)(2,1)S(1)} %fusion.3), channel_id=1, source_target_pairs={{0,4},{1,5},{2,6},{3,7},{4,0},{5,1},{6,2},{7,3},{8,12},{9,13},{10,... | collective-permute-start | bytes 276488 | tf_op jit(solution)/shard_map/ppermute | solution.py:277
